TPU v7x, 32 devices: a whole 2x2x4 slice. The times are simulated.
32 devices in a mesh: ep: 8 (over z, y), dp: 4 (over x, core).
Axes of the slice: x: 2, y: 2, z: 4, core: 2. Of those that a mesh axis runs over, the one named last changes fastest.
Arguments:
- tokens: bfloat16 [1024, 2048], P(('ep', 'dp')), may hold values from -6 to 6
- cotangent: bfloat16 [1024, 2048], P(('ep', 'dp')), may hold values from -6 to 6
- expert_ids: int32 [1024, 8], P(('ep', 'dp')), may hold values from 0 to 7, as said below
- route_weights: bfloat16 [1024, 8], P(('ep', 'dp')), may hold values from 0.049804688 to 0.5
- w_gate: bfloat16 [8, 2048, 768], P('ep'), may hold values from -0.125 to 0.125
- w_up: bfloat16 [8, 2048, 768], P('ep'), may hold values from -0.125 to 0.125
- w_down: bfloat16 [8, 768, 2048], P('ep'), may hold values from -0.21875 to 0.21875
Outputs:
- grad_tokens: bfloat16 [1024, 2048], P(('ep', 'dp'))
- grad_route: bfloat16 [1024, 8], P(('ep', 'dp'))
- grad_gate: bfloat16 [8, 2048, 768], P('ep', 'dp')
- grad_up: bfloat16 [8, 2048, 768], P('ep', 'dp')
- grad_down: bfloat16 [8, 768, 2048], P('ep', None, 'dp')
Inputs may be any that keep to these rules, and one draw needn't show every extreme that they name: `expert_ids`: each token names 8 different experts. The tokens of one device name no expert more than 32 times; 1 expert, drawn from the seed, are named exactly 32 times by every device's tokens.
All inputs are finite; a program needn't handle non-finite values.
Results may differ from a plain program's by a relative error of at most 0.0095.
Values may be sent and summed in bfloat16 or wider, within the bound.
A program may use at most 128 MiB of HBM per device.

v0:
```python
import jax
import jax.numpy as jnp
from jax import lax
from jax.experimental import pallas as pl
from jax.experimental.pallas import tpu as pltpu
from jax.sharding import PartitionSpec as P

block_rows = 128
contract_last = (((1,), (1,)), ((), ()))
contract_first = (((0,), (0,)), ((), ()))


def silu_parts(gate_pre):
    sig = jax.nn.sigmoid(gate_pre)
    return (gate_pre * sig, sig * (1.0 + gate_pre * (1.0 - sig)))


def expert_pass(rows_x, rows_cot, rows_w, live_count, w_gate_one, w_up_one, w_down_one):
    total, model = rows_x.shape
    width = w_gate_one.shape[1]

    def step(index, carry):
        acc_gate, acc_up, acc_down, slot_grad, route_grad = carry
        start = index * block_rows
        tok = lax.dynamic_slice_in_dim(rows_x, start, block_rows, 0)
        cot = lax.dynamic_slice_in_dim(rows_cot, start, block_rows, 0)
        weight = lax.dynamic_slice_in_dim(rows_w, start, block_rows, 0).astype(jnp.float32)[:, None]
        gate_pre = jnp.dot(tok, w_gate_one, preferred_element_type=jnp.float32)
        up_pre = jnp.dot(tok, w_up_one, preferred_element_type=jnp.float32)
        act, slope = silu_parts(gate_pre)
        hidden = lax.optimization_barrier((act * up_pre).astype(jnp.bfloat16))
        back = lax.dot_general(cot, w_down_one, contract_last, preferred_element_type=jnp.float32)
        route_part = jnp.sum(hidden.astype(jnp.float32) * back, axis=1)
        scaled = weight * back
        grad_gate_pre = (scaled * up_pre * slope).astype(jnp.bfloat16)
        grad_up_pre = (scaled * act).astype(jnp.bfloat16)
        scaled_cot = (weight * cot.astype(jnp.float32)).astype(jnp.bfloat16)
        part = lax.dot_general(
            grad_gate_pre, w_gate_one, contract_last, preferred_element_type=jnp.float32
        )
        part = part + lax.dot_general(
            grad_up_pre, w_up_one, contract_last, preferred_element_type=jnp.float32
        )
        acc_gate = acc_gate + lax.dot_general(
            tok, grad_gate_pre, contract_first, preferred_element_type=jnp.float32
        )
        acc_up = acc_up + lax.dot_general(
            tok, grad_up_pre, contract_first, preferred_element_type=jnp.float32
        )
        acc_down = acc_down + lax.dot_general(
            hidden, scaled_cot, contract_first, preferred_element_type=jnp.float32
        )
        slot_grad = lax.dynamic_update_slice_in_dim(slot_grad, part, start, 0)
        route_grad = lax.dynamic_update_slice_in_dim(route_grad, route_part, start, 0)
        return (acc_gate, acc_up, acc_down, slot_grad, route_grad)

    init = (
        jnp.zeros((model, width), jnp.float32),
        jnp.zeros((model, width), jnp.float32),
        jnp.zeros((width, model), jnp.float32),
        jnp.zeros((total, model), jnp.float32),
        jnp.zeros((total,), jnp.float32),
    )
    block_count = (live_count + block_rows - 1) // block_rows
    return lax.fori_loop(0, block_count, step, init)


def routed_body(tokens, cotangent, expert_ids, route_weights, w_gate, w_up, w_down):
    tok_count, topk = expert_ids.shape
    model = tokens.shape[1]
    experts = lax.axis_size("ep")
    capacity = min(tok_count, 2 * tok_count * topk // experts)
    slots = tok_count * topk
    row_total = experts * capacity
    flat_ids = expert_ids.reshape(slots)
    onehot = (flat_ids[:, None] == jnp.arange(experts, dtype=jnp.int32)[None, :]).astype(jnp.int32)
    position = jnp.sum((jnp.cumsum(onehot, axis=0) - 1) * onehot, axis=1)
    slot_ids = jnp.arange(slots, dtype=jnp.int32)
    source = (
        jnp.full((row_total,), slots, jnp.int32).at[flat_ids * capacity + position].set(slot_ids)
    )
    filled = source < slots
    source_token = jnp.where(filled, source // topk, tok_count)
    joined = jnp.concatenate([tokens, cotangent], axis=1)
    picked = jnp.take(joined, source_token, axis=0, mode="fill", fill_value=0)
    send_x = picked[:, :model].reshape(experts, capacity, model)
    send_cot = picked[:, model:].reshape(experts, capacity, model)
    send_w = jnp.take(
        route_weights.reshape(slots), jnp.where(filled, source, slots), mode="fill", fill_value=0
    ).reshape(experts, capacity)
    recv_x, recv_cot, recv_w = (
        lax.all_to_all(send_x, "ep", split_axis=0, concat_axis=0, tiled=True),
        lax.all_to_all(send_cot, "ep", split_axis=0, concat_axis=0, tiled=True),
        lax.all_to_all(send_w, "ep", split_axis=0, concat_axis=0, tiled=True),
    )
    flat_w = recv_w.reshape(row_total)
    live = (flat_w != 0).astype(jnp.int32)
    live_count = jnp.sum(live)
    place = jnp.where(live > 0, jnp.cumsum(live) - 1, row_total)
    anchor = (
        jnp.full((row_total,), row_total, jnp.int32)
        .at[place]
        .set(jnp.arange(row_total, dtype=jnp.int32), mode="drop")
    )
    recv_joined = jnp.concatenate(
        [recv_x.reshape(row_total, model), recv_cot.reshape(row_total, model)], axis=1
    )
    packed = jnp.take(recv_joined, anchor, axis=0, mode="fill", fill_value=0)
    pack_x = packed[:, :model]
    pack_cot = packed[:, model:]
    pack_w = jnp.take(flat_w, anchor, mode="fill", fill_value=0)
    w_gate_one = w_gate[0]
    w_up_one = w_up[0]
    w_down_one = w_down[0]
    acc_gate, acc_up, acc_down, slot_grad, route_grad = expert_pass(
        pack_x, pack_cot, pack_w, live_count, w_gate_one, w_up_one, w_down_one
    )
    slot_rows = jnp.take(slot_grad, place, axis=0, mode="fill", fill_value=0.0).astype(jnp.bfloat16)
    route_rows = jnp.take(route_grad, place, axis=0, mode="fill", fill_value=0.0).astype(
        jnp.bfloat16
    )
    back_x, back_route_rows = (
        lax.all_to_all(
            slot_rows.reshape(experts, capacity, model),
            "ep",
            split_axis=0,
            concat_axis=0,
            tiled=True,
        ),
        lax.all_to_all(
            route_rows.reshape(experts, capacity), "ep", split_axis=0, concat_axis=0, tiled=True
        ),
    )
    mine_rows = back_x[flat_ids, position].reshape(tok_count, topk, model)
    grad_tokens = jnp.sum(mine_rows.astype(jnp.float32), axis=1).astype(jnp.bfloat16)
    grad_route = back_route_rows[flat_ids, position].reshape(tok_count, topk)
    summed = (
        lax.psum_scatter(
            acc_gate[None].astype(jnp.bfloat16), "dp", scatter_dimension=1, tiled=True
        ).astype(jnp.float32),
        lax.psum_scatter(
            acc_up[None].astype(jnp.bfloat16), "dp", scatter_dimension=1, tiled=True
        ).astype(jnp.float32),
        lax.psum_scatter(
            acc_down[None].astype(jnp.bfloat16), "dp", scatter_dimension=2, tiled=True
        ).astype(jnp.float32),
    )
    return (
        grad_tokens,
        grad_route,
        summed[0].astype(jnp.bfloat16),
        summed[1].astype(jnp.bfloat16),
        summed[2].astype(jnp.bfloat16),
    )


def fused_kernel(
    tok_hbm, cot_hbm, ids_hbm, rw_hbm, wg_hbm, wu_hbm, wdn_hbm,
    gt_ref, route_ref, gg_ref, gu_ref, gd_ref,
    ids_ref, rw_ref, wg, wu, wdn, tc, wd, wbuf, cols, colst, act_buf, fac_buf, hid_buf, hw_own, hw_recv, gp_own, gp_recv,
    part, ys, yr, zs, zr, rs, rr,
    l_sem, w_send, w_recv, g_send, g_recv, c_send, c_recv,
    h_send, h_done, y_send, y_recv, z_send, z_recv, r_send, r_recv,
):
    ep_size = lax.axis_size("ep")
    groups = lax.axis_size("dp")
    count = tok_hbm.shape[0]
    col = tc.shape[3]
    tiles, rows, ft = hw_own.shape
    nz = ep_size // 2
    half = rows // 2
    ep = lax.axis_index("ep")
    dp = lax.axis_index("dp")
    z, y = ep // 2, ep % 2
    xx, core = dp // 2, dp % 2
    mine = y * nz + z
    ynb = z * 2 + 1 - y
    peers_dp = (xx * 2 + 1 - core, (1 - xx) * 2 + core, (1 - xx) * 2 + 1 - core)
    f32 = jnp.float32
    bf16 = jnp.bfloat16

    def span(index, size):
        return pl.ds(pl.multiple_of(index * size, size), size)

    def remote(src, dst, send, recv, ep_to, dp_to):
        return pltpu.make_async_remote_copy(
            src_ref=src, dst_ref=dst, send_sem=send, recv_sem=recv,
            device_id=(ep_to, dp_to), device_id_type=pl.DeviceIdType.MESH,
        )

    loads = [
        pltpu.make_async_copy(ref.at[:, pl.ds(j * col, col)], tc.at[k, j, span(mine, count)], l_sem.at[k, j])
        for k, ref in enumerate((tok_hbm, cot_hbm))
        for j in range(groups)
    ]
    for load in loads:
        load.start()
    lists = (
        pltpu.make_async_copy(ids_hbm, ids_ref, l_sem.at[3, 0]),
        pltpu.make_async_copy(rw_hbm, rw_ref, l_sem.at[3, 1]),
    )
    for load in lists:
        load.start()
    w_loads = [
        pltpu.make_async_copy(src, dst, l_sem.at[2, 1 + k])
        for k, (src, dst) in enumerate(((wg_hbm, wg), (wu_hbm, wu), (wdn_hbm, wdn)))
    ]

    barrier = pltpu.get_barrier_semaphore()
    for k in range(1, ep_size):
        pl.semaphore_signal(
            barrier, inc=1, device_id=((ep + k) % ep_size, dp), device_id_type=pl.DeviceIdType.MESH
        )
    for peer in peers_dp:
        pl.semaphore_signal(barrier, inc=1, device_id=(ep, peer), device_id_type=pl.DeviceIdType.MESH)
    wd[...] = jnp.zeros(wd.shape, f32)
    rs[...] = jnp.zeros(rs.shape, f32)
    for load in lists:
        load.wait()
    ids = ids_ref[...]
    values = rw_ref[...].astype(f32)
    for e in range(ep_size):
        line = jnp.sum(jnp.where(ids == e, values, 0.0), axis=0, keepdims=True)
        wd[e, :, 0:count] = jnp.broadcast_to(line, (wd.shape[1], count))
    pl.semaphore_wait(barrier, ep_size - 1 + len(peers_dp))

    def block(which, zz, yy):
        if which == 2:
            return cols.at[1, pl.ds(1, 2), span(yy * nz + zz, count)]
        return tc.at[which, :, span(yy * nz + zz, count)]

    def block_copy(which, way, zz, ep_to):
        view = block(which, zz, y)
        return remote(view, view, g_send.at[which, way, zz], g_recv.at[which, y * nz + zz], ep_to, dp)

    def send_up(which, zz):
        @pl.when(z + 1 < nz)
        def _():
            block_copy(which, 0, zz, ep + 2).start()

    def send_down(which, zz):
        @pl.when(z > 0)
        def _():
            block_copy(which, 1, zz, ep - 2).start()

    def send_side(which, zz):
        block_copy(which, 2, zz, ynb).start()

    def send_cols(which, pos, reach=3):
        if which == 2:
            return
        for r, peer in enumerate(peers_dp[:reach]):
            remote(
                tc.at[which, peer, span(pos, count)],
                cols.at[which, r, span(pos, count)],
                c_send.at[which, r], c_recv.at[which, r], ep, peer,
            ).start()

    def pass_on(which, d):
        @pl.when(z >= d)
        def _():
            block_copy(which, 0, z - d, ep).wait_recv()
            send_up(which, z - d)
            send_side(which, z - d)
            send_cols(which, y * nz + z - d, 3 - 2 * which)

        @pl.when(z + d < nz)
        def _():
            block_copy(which, 1, z + d, ep).wait_recv()
            send_down(which, z + d)
            send_side(which, z + d)
            send_cols(which, y * nz + z + d, 3 - 2 * which)

    def take_side(which):
        def take(k, carry):
            zz = (z + k) % nz
            pos = (1 - y) * nz + zz
            view = block(which, zz, 1 - y)
            remote(view, view, g_send.at[which, 2, zz], g_recv.at[which, pos], ep, dp).wait_recv()
            send_cols(which, pos, 3 - 2 * which)
            return carry

        lax.fori_loop(0, nz, take, 0)

    def h_copy(kind, r, t, forwarded=False):
        own, got = ((hw_own, hw_recv), (gp_own, gp_recv))[kind]
        src = got.at[1, t] if forwarded else own.at[t]
        peer = peers_dp[0] if forwarded else peers_dp[r]
        return remote(src, got.at[r, t], h_send.at[kind, r, t], h_done.at[kind, r, t], ep, peer)

    def forward(kind, t):
        h_copy(kind, 1, t).wait_recv()
        h_copy(kind, 2, t, True).start()

    for which in range(2):
        for load in loads[which * groups:(which + 1) * groups]:
            load.wait()
        send_up(which, z)
        send_down(which, z)
        send_side(which, z)
        send_cols(which, mine)
    wbuf[mine] = wd[ep]
    for k in range(1, ep_size):
        to = (ep + k) % ep_size
        remote(wd.at[to], wbuf.at[mine], w_send.at[k], w_recv.at[mine], to, dp).start()
    for load in w_loads:
        load.start()
    for d in range(1, nz):
        pass_on(0, d)
    take_side(0)
    for k in range(1, ep_size):
        frm = (ep + k) % ep_size
        pos = (frm % 2) * nz + frm // 2
        remote(wd.at[frm], wbuf.at[pos], w_send.at[k], w_recv.at[pos], ep, dp).wait_recv()
    for load in w_loads:
        load.wait()
    flat = wbuf[...].reshape(ep_size * wbuf.shape[1], wbuf.shape[2])
    turned = jnp.concatenate([flat] * (128 // flat.shape[0]), axis=0).T
    step = wbuf.shape[1]
    weight = jnp.concatenate([turned[0:count, p * step:p * step + 1] for p in range(ep_size)], axis=0)

    for t in range(max(tiles, nz - 1)):
        if t < nz - 1:
            pass_on(1, t + 1)
        if t < tiles:
            lanes = pl.ds(t * ft, ft)
            gate_pre = jnp.zeros((rows, ft), f32)
            up_pre = jnp.zeros((rows, ft), f32)
            for j in range(groups):
                depth = pl.ds(j * col, col)
                gate_pre += jnp.dot(tc[0, j], wg[depth, lanes], preferred_element_type=f32)
                up_pre += jnp.dot(tc[0, j], wu[depth, lanes], preferred_element_type=f32)
            act, slope = silu_parts(gate_pre)
            product = act * up_pre
            hw_own[t] = (weight * product).astype(bf16)
            act_buf[t] = act
            fac_buf[t] = up_pre * slope
            hid_buf[t] = product.astype(bf16)
            for r in (1, 0):
                h_copy(0, r, t).start()
    for r in (1, 2):
        view = cols.at[1, r, span(mine, count)]
        remote(view, view, c_send.at[1, r], c_recv.at[1, r], ep, peers_dp[r]).wait_recv()
    send_up(2, z)
    send_down(2, z)
    take_side(1)
    send_side(2, z)
    pass_on(2, 1)

    def back_step(t, route):
        back = jnp.zeros((rows, ft), f32)
        for j in range(groups):
            back += lax.dot_general(
                tc[1, j], wdn[span(t, ft), pl.ds(j * col, col)], contract_last, preferred_element_type=f32
            )
        scaled = weight * back
        gp_own[t, 0] = (scaled * fac_buf[t]).astype(bf16)
        gp_own[t, 1] = (scaled * act_buf[t]).astype(bf16)
        route = route + jnp.sum(hid_buf[t].astype(f32) * back, axis=1, keepdims=True)
        for r in (1, 0):
            h_copy(1, r, t).start()
        return route

    route = lax.fori_loop(0, tiles, back_step, jnp.zeros((rows, 1), f32))
    for d in range(2, nz):
        pass_on(2, d)
    lined = jnp.broadcast_to(route, (rows, 128)).T
    for p in range(ep_size):
        line = lined[0:1, p * count:(p + 1) * count]
        rs[p, :, 0:count] = jnp.broadcast_to(line, (rs.shape[1], count))

    def slot_step(n, carry):
        total = jnp.zeros((rows, col), f32)
        for t in range(tiles):
            lanes = pl.ds(t * ft, ft)
            total += lax.dot_general(gp_own[t, 0], wg[span(n, col), lanes], contract_last, preferred_element_type=f32)
            total += lax.dot_general(gp_own[t, 1], wu[span(n, col), lanes], contract_last, preferred_element_type=f32)
        part[n] = total.reshape(2, half, col)
        ys[n] = part[n, 1 - y].astype(bf16)
        remote(ys.at[n], yr.at[n], y_send.at[n], y_recv.at[n], ynb, dp).start()
        return carry

    lax.fori_loop(0, groups, slot_step, 0)
    for k in range(1, ep_size):
        to = (ep + k) % ep_size
        pos = (to % 2) * nz + to // 2
        remote(rs.at[pos], rr.at[ep], r_send.at[k], r_recv.at[ep], to, dp).start()
    rr[ep] = rs[mine]
    for t in range(tiles):
        forward(0, t)

    def add_step(n, carry):
        remote(ys.at[n], yr.at[n], y_send.at[n], y_recv.at[n], ynb, dp).wait()
        total = part[n, y] + yr[n].astype(f32)
        part[n, y] = total
        zs[n] = total.astype(bf16)
        for k in range(1, nz):
            to = (z + k) % nz
            remote(
                zs.at[n, span(to, count)], zr.at[n, k - 1], z_send.at[n, k - 1], z_recv.at[n, k - 1], to * 2 + y, dp
            ).start()
        return carry

    lax.fori_loop(0, groups, add_step, 0)
    colst[0] = tc[0, dp].T
    for r in range(3):
        remote(cols.at[0, r], cols.at[0, r], c_send.at[0, r], c_recv.at[0, r], ep, peers_dp[r]).wait_recv()
        colst[1 + r] = cols[0, r].T
    remote(cols.at[1, 0], cols.at[1, 0], c_send.at[1, 0], c_recv.at[1, 0], ep, peers_dp[0]).wait_recv()
    take_side(2)
    forward(1, 0)

    def down_step(t, carry):
        for r in (0, 2):
            h_copy(0, r, t).wait_recv()
        blocks = [hw_own.at[t]] + [hw_recv.at[r, t] for r in range(3)]
        cots = [tc.at[1, dp]] + [cols.at[1, r] for r in range(3)]
        grad_down = jnp.zeros((ft, col), f32)
        for g in range(4):
            grad_down += lax.dot_general(blocks[g][...], cots[g][...], contract_first, preferred_element_type=f32)
        gd_ref[span(t, ft), :] = grad_down.astype(bf16)
        return carry

    lax.fori_loop(0, tiles, down_step, 0)

    def sum_step(n, carry):
        total = part[n, y, span(z, count), :]
        for k in range(1, nz):
            remote(
                zs.at[n, pl.ds(0, count)], zr.at[n, k - 1], z_send.at[n, k - 1], z_recv.at[n, k - 1], ep, dp
            ).wait()
            total = total + zr[n, k - 1].astype(f32)
        gt_ref[:, span(n, col)] = total.astype(bf16)
        return carry

    def weight_step(t, carry):
        @pl.when(t + 1 < tiles)
        def _():
            forward(1, t + 1)

        @pl.when(t + 1 == tiles)
        def _():
            lax.fori_loop(0, groups, sum_step, 0)

        for r in (0, 2):
            h_copy(1, r, t).wait_recv()
        blocks = [gp_own.at[t]] + [gp_recv.at[r, t] for r in range(3)]
        grad_gate = jnp.zeros((col, ft), f32)
        grad_up = jnp.zeros((col, ft), f32)
        for g in range(4):
            grad_gate += jnp.dot(colst[g], blocks[g][0], preferred_element_type=f32)
            grad_up += jnp.dot(colst[g], blocks[g][1], preferred_element_type=f32)
        gg_ref[:, span(t, ft)] = grad_gate.astype(bf16)
        gu_ref[:, span(t, ft)] = grad_up.astype(bf16)
        return carry

    lax.fori_loop(0, tiles, weight_step, 0)

    for k in range(1, ep_size):
        frm = (ep + k) % ep_size
        remote(rs.at[0], rr.at[frm], r_send.at[k], r_recv.at[frm], ep, dp).wait()
        remote(wd.at[0], wbuf.at[mine], w_send.at[k], w_recv.at[mine], ep, dp).wait_send()
    table = jnp.zeros(ids.shape, f32)
    for e in range(ep_size):
        table = table + jnp.where(ids == e, rr[e, 0:1, 0:count], 0.0)
    route_ref[...] = table.astype(bf16)
    for which in range(3):
        for zz in range(nz):
            block_copy(which, 2, zz, ep).wait_send()

            @pl.when(jnp.logical_and(z >= zz, z + 1 < nz))
            def _():
                block_copy(which, 0, zz, ep).wait_send()

            @pl.when(jnp.logical_and(z <= zz, z > 0))
            def _():
                block_copy(which, 1, zz, ep).wait_send()

    for which in range(2):
        for r in range(3):
            view = cols.at[1, r, span(mine, count)] if which == 1 and r > 0 else cols.at[which, r]
            remote(view, view, c_send.at[which, r], c_recv.at[which, r], ep, peers_dp[r]).wait_send()
        for t in range(tiles):
            for r in range(3):
                h_copy(which, r, t).wait_send()


def store_kernel(*refs):
    sems = refs[-1]
    each = (len(refs) - 1) // 2
    copies = [pltpu.make_async_copy(refs[k], refs[each + k], sems.at[k]) for k in range(each)]
    for copy in copies:
        copy.start()
    for copy in copies:
        copy.wait()


def fused_body(tokens, cotangent, expert_ids, route_weights, w_gate, w_up, w_down):
    count, topk = expert_ids.shape
    model = tokens.shape[1]
    experts = lax.axis_size("ep")
    groups = lax.axis_size("dp")
    width = w_gate.shape[2]
    rows = experts * count
    col = model // groups
    ft = 256 if width % 256 == 0 else width
    tiles = width // ft
    lanes = 128
    bf16 = jnp.bfloat16
    f32 = jnp.float32
    any_spec = pl.BlockSpec(memory_space=pl.ANY)
    hbm = pl.BlockSpec(memory_space=pltpu.HBM)
    vmem = pl.BlockSpec(memory_space=pltpu.VMEM)
    dma = pltpu.SemaphoreType.DMA
    nz = experts // 2
    small = (experts, 8, lanes)
    shapes = ((count, model), (topk, count), (col, width), (col, width), (width, col))
    outs = pl.pallas_call(
        fused_kernel,
        name="fused_layer",
        out_shape=tuple(pltpu.VMEM(shape, bf16) for shape in shapes),
        in_specs=[hbm] * 7,
        out_specs=(vmem,) * 5,
        scratch_shapes=[
            pltpu.VMEM((topk, count), jnp.int32),
            pltpu.VMEM((topk, count), bf16),
            pltpu.VMEM((model, width), bf16),
            pltpu.VMEM((model, width), bf16),
            pltpu.VMEM((width, model), bf16),
            pltpu.VMEM((2, groups, rows, col), bf16),
            pltpu.VMEM(small, f32),
            pltpu.VMEM(small, f32),
            pltpu.VMEM((2, 3, rows, col), bf16),
            pltpu.VMEM((4, col, rows), bf16),
            pltpu.VMEM((tiles, rows, ft), f32),
            pltpu.VMEM((tiles, rows, ft), f32),
            pltpu.VMEM((tiles, rows, ft), bf16),
            pltpu.VMEM((tiles, rows, ft), bf16),
            pltpu.VMEM((3, tiles, rows, ft), bf16),
            pltpu.VMEM((tiles, 2, rows, ft), bf16),
            pltpu.VMEM((3, tiles, 2, rows, ft), bf16),
            pltpu.VMEM((groups, 2, rows // 2, col), f32),
            pltpu.VMEM((groups, rows // 2, col), bf16),
            pltpu.VMEM((groups, rows // 2, col), bf16),
            pltpu.VMEM((groups, rows // 2, col), bf16),
            pltpu.VMEM((groups, nz - 1, count, col), bf16),
            pltpu.VMEM(small, f32),
            pltpu.VMEM(small, f32),
            dma((4, max(groups, 4))),
            dma((experts,)),
            dma((experts,)),
            dma((3, 3, nz)),
            dma((3, experts)),
            dma((2, 3)),
            dma((2, 3)),
            dma((2, 3, tiles)),
            dma((2, 3, tiles)),
            dma((groups,)),
            dma((groups,)),
            dma((groups, nz - 1)),
            dma((groups, nz - 1)),
            dma((experts,)),
            dma((experts,)),
        ],
        compiler_params=pltpu.CompilerParams(
            collective_id=0, has_side_effects=True, vmem_limit_bytes=64200000
        ),
    )(tokens, cotangent, expert_ids.T, route_weights.T, w_gate[0], w_up[0], w_down[0])
    outs = pl.pallas_call(
        store_kernel,
        name="store_results",
        out_shape=tuple(jax.ShapeDtypeStruct(shape, bf16) for shape in shapes),
        in_specs=[any_spec] * 5,
        out_specs=(any_spec,) * 5,
        scratch_shapes=[dma((5,))],
        compiler_params=pltpu.CompilerParams(vmem_limit_bytes=4 * 1024 * 1024),
    )(*outs)
    grad_tokens, grad_route, grad_gate, grad_up, grad_down = outs
    return grad_tokens, grad_route.T, grad_gate[None], grad_up[None], grad_down[None]


def body(tokens, cotangent, expert_ids, route_weights, w_gate, w_up, w_down):
    tok_count, topk = expert_ids.shape
    experts = lax.axis_size("ep")
    whole = 2 * tok_count * topk // experts >= tok_count
    paired = lax.axis_size("dp") == 4 and experts in (4, 8, 16) and tok_count in (16, 32, 64, 128)
    chosen = fused_body if whole and paired else routed_body
    return chosen(tokens, cotangent, expert_ids, route_weights, w_gate, w_up, w_down)


def solution(mesh):
    return jax.shard_map(
        body,
        mesh=mesh,
        in_specs=(
            P(("ep", "dp"), None),
            P(("ep", "dp"), None),
            P(("ep", "dp"), None),
            P(("ep", "dp"), None),
            P("ep", None, None),
            P("ep", None, None),
            P("ep", None, None),
        ),
        out_specs=(
            P(("ep", "dp"), None),
            P(("ep", "dp"), None),
            P("ep", "dp", None),
            P("ep", "dp", None),
            P("ep", None, "dp"),
        ),
        check_vma=False,
    )
```

profile of v0, /device:TPU:0, one launch (start us, length us, event | category | flops | bytes accessed | tf_op | source)
XLA Modules:
  0.0 60.6 jit_solution(14149647554084327244)
XLA Ops:
  0.6 58.5 %fused_layer.1 = (bf16[32,2048]{1,0:T(8,128)(2,1)S(1)}, bf16[8,32]{1,0:T(8,128)(2,1)S(1)}, bf16[512,768]{1,0:T(8,128)(2,1)S(1)}, bf16[512,768]{1,0:T(8,128)(2,1)S(1)}, bf16[768,512]{1,0:T(8,128)(2,1)S(1)}) custom-call(bf16[32,2048]{1,0:T(8,128)(2,1)} %tok_hbm.1, bf16[32,2048]{1,0:T(8,128)(2,1)} %cot_hbm.1, s32[8,32]{1,0:T(8,128)} %bitcast.12, ...), custom_call_target="tpu_custom_call" | custom-call | tf_op jit(solution)/shard_map/fused_layer/pallas_call | solution.py:518
  59.1 1.5 %store_results.1 = (bf16[32,2048]{1,0:T(8,128)(2,1)}, bf16[8,32]{1,0:T(8,128)(2,1)}, bf16[512,768]{1,0:T(8,128)(2,1)}, bf16[512,768]{1,0:T(8,128)(2,1)}, bf16[768,512]{1,0:T(8,128)(2,1)}) custom-call(bf16[32,2048]{1,0:T(8,128)(2,1)S(1)} %get-tuple-element.15.refs_0_, bf16[8,32]{1,0:T(8,128)(2,1)S(1)} %get-tuple-element.16.refs_1_, ...), custom_call_target="tpu_custom_call" | custom-call | tf_op jit(solution)/shard_map/store_results/pallas_call | solution.py:569
where the time goes:
time: 60.8 us; the launch traced here: 60.6 us
  Pallas kernels  59.9 us (99%)
  between operations  0.64 us (1%)
    pallas_call x1, Pallas kernels, fused_body(): pl.pallas_call(fused_kernel, name='fused_layer', out_shape=tuple((pltpu.V...  58.5 us
    pallas_call x1, Pallas kernels, fused_body(): pl.pallas_call(store_kernel, name='store_results', out_shape=tuple((jax.S...  1.49 us

commit v1 on v0

--- a/solution.py
+++ b/solution.py
@@ -157,27 +157,37 @@
 def fused_kernel(
     tok_hbm, cot_hbm, ids_hbm, rw_hbm, wg_hbm, wu_hbm, wdn_hbm,
     gt_ref, route_ref, gg_ref, gu_ref, gd_ref,
-    ids_ref, rw_ref, wg, wu, wdn, tc, wd, wbuf, cols, colst, act_buf, fac_buf, hid_buf, hw_own, hw_recv, gp_own, gp_recv,
-    part, ys, yr, zs, zr, rs, rr,
-    l_sem, w_send, w_recv, g_send, g_recv, c_send, c_recv,
-    h_send, h_done, y_send, y_recv, z_send, z_recv, r_send, r_recv,
+    ids_ref, rw_ref, wg, wu, wdn, tc, wd, wbuf, wcol, cols, colst, act_buf, fac_buf, hid_buf,
+    hw_own, hw_recv, gp_own, gp_recv, part, ys, yr, zs, zr, xs, xr, rs, rr,
+    l_sem, w_sem, g_send, g_recv, c_send, c_recv, h_send, h_done, y_sem, z_sem, x_sem, r_sem,
 ):
     ep_size = lax.axis_size("ep")
     groups = lax.axis_size("dp")
     count = tok_hbm.shape[0]
     col = tc.shape[3]
     tiles, rows, ft = hw_own.shape
-    nz = ep_size // 2
     half = rows // 2
     ep = lax.axis_index("ep")
     dp = lax.axis_index("dp")
     z, y = ep // 2, ep % 2
+    q, i = z // 2, z % 2
     xx, core = dp // 2, dp % 2
-    mine = y * nz + z
+    peers_dp = (xx * 2 + 1 - core, (1 - xx) * 2 + core, (1 - xx) * 2 + 1 - core)
+    inner = i != q
+    outer = i == q
+    zp = z + 1 - 2 * i
     ynb = z * 2 + 1 - y
-    peers_dp = (xx * 2 + 1 - core, (1 - xx) * 2 + core, (1 - xx) * 2 + 1 - core)
+    znb = zp * 2 + y
+    diag = zp * 2 + 1 - y
+    near = (2 - q) * 2 + y
+    far = (3 - 3 * q) * 2 + y
+    near_o = (2 - q) * 2 + 1 - y
+    far_o = (3 - 3 * q) * 2 + 1 - y
+    twin = (ep + 4) % 8
+    pairs = (q, 1 - q)
     f32 = jnp.float32
     bf16 = jnp.bfloat16
+    first = 1
 
     def span(index, size):
         return pl.ds(pl.multiple_of(index * size, size), size)
@@ -189,20 +199,23 @@
         )
 
     loads = [
-        pltpu.make_async_copy(ref.at[:, pl.ds(j * col, col)], tc.at[k, j, span(mine, count)], l_sem.at[k, j])
+        [
+            pltpu.make_async_copy(ref.at[:, pl.ds(j * col, col)], tc.at[k, j, span(ep, count)], l_sem.at[k])
+            for j in range(groups)
+        ]
         for k, ref in enumerate((tok_hbm, cot_hbm))
-        for j in range(groups)
     ]
-    for load in loads:
-        load.start()
+    for group in loads:
+        for load in group:
+            load.start()
     lists = (
-        pltpu.make_async_copy(ids_hbm, ids_ref, l_sem.at[3, 0]),
-        pltpu.make_async_copy(rw_hbm, rw_ref, l_sem.at[3, 1]),
+        pltpu.make_async_copy(ids_hbm, ids_ref, l_sem.at[2]),
+        pltpu.make_async_copy(rw_hbm, rw_ref, l_sem.at[3]),
     )
     for load in lists:
         load.start()
     w_loads = [
-        pltpu.make_async_copy(src, dst, l_sem.at[2, 1 + k])
+        pltpu.make_async_copy(src, dst, l_sem.at[4 + k])
         for k, (src, dst) in enumerate(((wg_hbm, wg), (wu_hbm, wu), (wdn_hbm, wdn)))
     ]
 
@@ -224,195 +237,301 @@
         wd[e, :, 0:count] = jnp.broadcast_to(line, (wd.shape[1], count))
     pl.semaphore_wait(barrier, ep_size - 1 + len(peers_dp))
 
-    def block(which, zz, yy):
-        if which == 2:
-            return cols.at[1, pl.ds(1, 2), span(yy * nz + zz, count)]
-        return tc.at[which, :, span(yy * nz + zz, count)]
-
-    def block_copy(which, way, zz, ep_to):
-        view = block(which, zz, y)
-        return remote(view, view, g_send.at[which, way, zz], g_recv.at[which, y * nz + zz], ep_to, dp)
-
-    def send_up(which, zz):
-        @pl.when(z + 1 < nz)
+    def view(k, pos, piece):
+        if k == 2:
+            return cols.at[1, pl.ds((1, 1, 2)[piece], (2, 1, 1)[piece]), span(pos, count)]
+        return tc.at[k, pl.ds((0, 0, first)[piece], (groups, first, groups - first)[piece]), span(pos, count)]
+
+    def hop(k, pos, piece, late, ep_to):
+        ref = view(k, pos, piece)
+        slot = ep_to if piece == 2 else pos
+        remote(ref, ref, g_send.at[k, late], g_recv.at[k, slot], ep_to, dp).start()
+
+    def got(k, pos):
+        ref = view(k, pos, 0)
+        remote(ref, ref, g_send.at[k, 0], g_recv.at[k, pos], ynb, dp).wait_recv()
+
+    def got_diag(k):
+        ref = view(k, diag, 1)
+        remote(ref, ref, g_send.at[k, 0], g_recv.at[k, diag], ynb, dp).wait_recv()
+        ref = view(k, diag, 2)
+        remote(ref, ref, g_send.at[k, 0], g_recv.at[k, ep], znb, dp).wait_recv()
+
+    def send_cols(k, pos, reach):
+        for r in (1, 2, 0)[3 - reach:] if reach == 3 else (0,):
+            peer = peers_dp[r]
+            remote(
+                tc.at[k, peer, span(pos, count)], cols.at[k, r, span(pos, count)],
+                c_send.at[k, r], c_recv.at[k, r], ep, peer,
+            ).start()
+
+    def share(k, pos):
+        if k < 2:
+            send_cols(k, pos, 3 - 2 * k)
+
+    def own_out(k):
+        hop(k, ep, 0, 0, ynb)
+        hop(k, ep, 0, 0, znb)
+
+        @pl.when(inner)
         def _():
-            block_copy(which, 0, zz, ep + 2).start()
-
-    def send_down(which, zz):
-        @pl.when(z > 0)
+            hop(k, ep, 0, 1, near)
+
+    def pair_out(k):
+        got(k, znb)
+        hop(k, znb, 1, 0, ynb)
+
+        @pl.when(inner)
         def _():
-            block_copy(which, 1, zz, ep - 2).start()
-
-    def send_side(which, zz):
-        block_copy(which, 2, zz, ynb).start()
-
-    def send_cols(which, pos, reach=3):
-        if which == 2:
-            return
-        for r, peer in enumerate(peers_dp[:reach]):
-            remote(
-                tc.at[which, peer, span(pos, count)],
-                cols.at[which, r, span(pos, count)],
-                c_send.at[which, r], c_recv.at[which, r], ep, peer,
-            ).start()
-
-    def pass_on(which, d):
-        @pl.when(z >= d)
+            hop(k, znb, 0, 1, near)
+
+        share(k, znb)
+        got(k, ynb)
+        hop(k, ynb, 2, 0, znb)
+        share(k, ynb)
+
+    def inner_pass(k, pos):
+        @pl.when(inner)
         def _():
-            block_copy(which, 0, z - d, ep).wait_recv()
-            send_up(which, z - d)
-            send_side(which, z - d)
-            send_cols(which, y * nz + z - d, 3 - 2 * which)
-
-        @pl.when(z + d < nz)
+            got(k, pos)
+            hop(k, pos, 0, 1, znb)
+            hop(k, pos, 0, 1, ynb)
+            share(k, pos)
+
+    def outer_pass(k, pos):
+        @pl.when(outer)
         def _():
-            block_copy(which, 1, z + d, ep).wait_recv()
-            send_down(which, z + d)
-            send_side(which, z + d)
-            send_cols(which, y * nz + z + d, 3 - 2 * which)
-
-    def take_side(which):
-        def take(k, carry):
-            zz = (z + k) % nz
-            pos = (1 - y) * nz + zz
-            view = block(which, zz, 1 - y)
-            remote(view, view, g_send.at[which, 2, zz], g_recv.at[which, pos], ep, dp).wait_recv()
-            send_cols(which, pos, 3 - 2 * which)
-            return carry
-
-        lax.fori_loop(0, nz, take, 0)
-
-    def h_copy(kind, r, t, forwarded=False):
-        own, got = ((hw_own, hw_recv), (gp_own, gp_recv))[kind]
-        src = got.at[1, t] if forwarded else own.at[t]
-        peer = peers_dp[0] if forwarded else peers_dp[r]
-        return remote(src, got.at[r, t], h_send.at[kind, r, t], h_done.at[kind, r, t], ep, peer)
-
-    def forward(kind, t):
-        h_copy(kind, 1, t).wait_recv()
-        h_copy(kind, 2, t, True).start()
-
-    for which in range(2):
-        for load in loads[which * groups:(which + 1) * groups]:
-            load.wait()
-        send_up(which, z)
-        send_down(which, z)
-        send_side(which, z)
-        send_cols(which, mine)
-    wbuf[mine] = wd[ep]
+            got(k, pos)
+            hop(k, pos, 0, 1, ynb)
+            share(k, pos)
+
+    def take(k, pos):
+        got(k, pos)
+        share(k, pos)
+
+    for k in range(2):
+        ref = view(k, ep, 0)
+        pltpu.make_async_copy(ref, ref, l_sem.at[k]).wait()
+        own_out(k)
+        send_cols(k, ep, 3)
     for k in range(1, ep_size):
         to = (ep + k) % ep_size
-        remote(wd.at[to], wbuf.at[mine], w_send.at[k], w_recv.at[mine], to, dp).start()
+        remote(wd.at[to], wbuf.at[ep], w_sem.at[0], w_sem.at[1], to, dp).start()
+    keep_w = pltpu.make_async_copy(wd.at[ep], wbuf.at[ep], w_sem.at[1])
+    keep_w.start()
     for load in w_loads:
         load.start()
-    for d in range(1, nz):
-        pass_on(0, d)
-    take_side(0)
-    for k in range(1, ep_size):
-        frm = (ep + k) % ep_size
-        pos = (frm % 2) * nz + frm // 2
-        remote(wd.at[frm], wbuf.at[pos], w_send.at[k], w_recv.at[pos], ep, dp).wait_recv()
+    pair_out(0)
+    pair_out(1)
+
+    def wave_rows(wave):
+        return span(pairs[wave], half)
+
+    def gate_step(wave):
+        block = wave_rows(wave)
+
+        def step(t, carry):
+            lanes = span(t, ft)
+            gate_pre = jnp.zeros((half, ft), f32)
+            up_pre = jnp.zeros((half, ft), f32)
+            for j in range(groups):
+                depth = pl.ds(j * col, col)
+                gate_pre += jnp.dot(tc[0, j, block], wg[depth, lanes], preferred_element_type=f32)
+                up_pre += jnp.dot(tc[0, j, block], wu[depth, lanes], preferred_element_type=f32)
+            act, slope = silu_parts(gate_pre)
+            product = act * up_pre
+            weight = wcol[block, 0:1]
+            hw_own[t, block] = (weight * product).astype(bf16)
+            act_buf[t, block] = act
+            fac_buf[t, block] = up_pre * slope
+            hid_buf[t, block] = product.astype(bf16)
+            for r in (1, 0):
+                done = h_done.at[1 + wave] if r == 1 else h_done.at[0]
+                remote(
+                    hw_own.at[t, block], hw_recv.at[r, t, block], h_send.at[0, r], done, ep, peers_dp[r]
+                ).start()
+            return carry
+
+        lax.fori_loop(0, tiles, step, 0)
+
+    def back_step(wave):
+        block = wave_rows(wave)
+        weight = wcol[block, 0:1]
+
+        def step(t, route):
+            back = jnp.zeros((half, ft), f32)
+            for j in range(groups):
+                back += lax.dot_general(
+                    tc[1, j, block], wdn[span(t, ft), pl.ds(j * col, col)], contract_last, preferred_element_type=f32
+                )
+            scaled = weight * back
+            gp_own[t, 0, block] = (scaled * fac_buf[t, block]).astype(bf16)
+            gp_own[t, 1, block] = (scaled * act_buf[t, block]).astype(bf16)
+            route = route + jnp.sum(hid_buf[t, block].astype(f32) * back, axis=1, keepdims=True)
+            for r in (1, 0):
+                done = h_done.at[(5 + wave) + wave * t] if r == 1 else h_done.at[4]
+                remote(
+                    gp_own.at[t, :, block], gp_recv.at[r, t, :, block], h_send.at[1, r], done, ep, peers_dp[r]
+                ).start()
+            return route
+
+        route = lax.fori_loop(0, tiles, step, jnp.zeros((half, 1), f32))
+        lined = jnp.broadcast_to(route, (half, 128)).T
+        for p in range(4):
+            line = lined[0:1, p * count:(p + 1) * count]
+            rs[pairs[wave] * 4 + p, :, 0:count] = jnp.broadcast_to(line, (rs.shape[1], count))
+
+    def y_copy(wave, n):
+        done = y_sem.at[1 + wave * (1 + n)]
+        return remote(ys.at[wave, n], yr.at[wave, n], y_sem.at[0], done, ynb, dp)
+
+    def slot_step(wave, sending):
+        block = wave_rows(wave)
+
+        def step(n, carry):
+            total = jnp.zeros((half, col), f32)
+            for t in range(tiles):
+                lanes = pl.ds(t * ft, ft)
+                total += lax.dot_general(
+                    gp_own[t, 0, block], wg[span(n, col), lanes], contract_last, preferred_element_type=f32
+                )
+                total += lax.dot_general(
+                    gp_own[t, 1, block], wu[span(n, col), lanes], contract_last, preferred_element_type=f32
+                )
+            part[wave, n] = total.reshape(2, 2, count, col)
+            ys[wave, n] = part[wave, n, :, 1 - y].astype(bf16)
+            if sending is None:
+                y_copy(wave, n).start()
+            else:
+                @pl.when(sending)
+                def _():
+                    y_copy(wave, n).start()
+            return carry
+
+        lax.fori_loop(0, groups, step, 0)
+
+    def y_add(wave):
+        if wave == 0:
+            remote(ys.at[0], yr.at[0], y_sem.at[0], y_sem.at[1], ynb, dp).wait_recv()
+
+        def step(n, carry):
+            if wave == 1:
+                y_copy(1, n).wait_recv()
+            total = part[wave, n, :, y] + yr[wave, n].astype(f32)
+            part[wave, n, :, y] = total
+            zs[wave, n] = part[wave, n, 1 - i, y].astype(bf16)
+            remote(
+                zs.at[wave, n], zr.at[wave, n], z_sem.at[0], z_sem.at[1 + wave * (1 + n)], znb, dp
+            ).start()
+            return carry
+
+        lax.fori_loop(0, groups, step, 0)
+
+    def z_add(wave):
+        if wave == 0:
+            remote(zs.at[0], zr.at[0], z_sem.at[0], z_sem.at[1], znb, dp).wait_recv()
+
+        def step(n, carry):
+            if wave == 1:
+                remote(zs.at[1, n], zr.at[1, n], z_sem.at[0], z_sem.at[2 + n], znb, dp).wait_recv()
+            total = part[wave, n, i, y] + zr[wave, n].astype(f32)
+            if wave == 0:
+                part[0, n, i, y] = total
+            else:
+                xs[n] = total.astype(bf16)
+                remote(xs.at[n], xr.at[n], x_sem.at[0], x_sem.at[1 + n], twin, dp).start()
+            return carry
+
+        lax.fori_loop(0, groups, step, 0)
+
+    def pass_hidden(wave):
+        block = wave_rows(wave)
+        ref = hw_recv.at[1, :, block]
+        remote(ref, ref, h_send.at[0, 1], h_done.at[1 + wave], ep, peers_dp[1]).wait_recv()
+        remote(ref, hw_recv.at[2, :, block], h_send.at[0, 2], h_done.at[3], ep, peers_dp[0]).start()
+
+    def pass_grad_first():
+        ref = gp_recv.at[1, :, :, wave_rows(0)]
+        remote(ref, ref, h_send.at[1, 1], h_done.at[5], ep, peers_dp[1]).wait_recv()
+        remote(ref, gp_recv.at[2, :, :, wave_rows(0)], h_send.at[1, 2], h_done.at[6 + tiles], ep, peers_dp[0]).start()
+
+    def pass_grad(t):
+        ref = gp_recv.at[1, t, :, wave_rows(1)]
+        remote(ref, ref, h_send.at[1, 1], h_done.at[6 + t], ep, peers_dp[1]).wait_recv()
+        remote(
+            ref, gp_recv.at[2, t, :, wave_rows(1)], h_send.at[1, 2], h_done.at[7 + tiles + t], ep, peers_dp[0]
+        ).start()
+
+    got_diag(0)
+    share(0, diag)
     for load in w_loads:
         load.wait()
+    remote(wbuf, wbuf, w_sem.at[0], w_sem.at[1], ynb, dp).wait_recv()
     flat = wbuf[...].reshape(ep_size * wbuf.shape[1], wbuf.shape[2])
     turned = jnp.concatenate([flat] * (128 // flat.shape[0]), axis=0).T
-    step = wbuf.shape[1]
-    weight = jnp.concatenate([turned[0:count, p * step:p * step + 1] for p in range(ep_size)], axis=0)
-
-    for t in range(max(tiles, nz - 1)):
-        if t < nz - 1:
-            pass_on(1, t + 1)
-        if t < tiles:
-            lanes = pl.ds(t * ft, ft)
-            gate_pre = jnp.zeros((rows, ft), f32)
-            up_pre = jnp.zeros((rows, ft), f32)
-            for j in range(groups):
-                depth = pl.ds(j * col, col)
-                gate_pre += jnp.dot(tc[0, j], wg[depth, lanes], preferred_element_type=f32)
-                up_pre += jnp.dot(tc[0, j], wu[depth, lanes], preferred_element_type=f32)
-            act, slope = silu_parts(gate_pre)
-            product = act * up_pre
-            hw_own[t] = (weight * product).astype(bf16)
-            act_buf[t] = act
-            fac_buf[t] = up_pre * slope
-            hid_buf[t] = product.astype(bf16)
-            for r in (1, 0):
-                h_copy(0, r, t).start()
+    step8 = wbuf.shape[1]
+    for p in range(ep_size):
+        wcol[pl.ds(p * count, count), :] = jnp.broadcast_to(turned[0:count, p * step8:p * step8 + 1], (count, 128))
+    gate_step(0)
+    inner_pass(0, near)
+    inner_pass(0, far)
+    inner_pass(1, near)
+    got_diag(1)
+    share(1, diag)
+    back_step(0)
+    inner_pass(1, far)
     for r in (1, 2):
-        view = cols.at[1, r, span(mine, count)]
-        remote(view, view, c_send.at[1, r], c_recv.at[1, r], ep, peers_dp[r]).wait_recv()
-    send_up(2, z)
-    send_down(2, z)
-    take_side(1)
-    send_side(2, z)
-    pass_on(2, 1)
-
-    def back_step(t, route):
-        back = jnp.zeros((rows, ft), f32)
-        for j in range(groups):
-            back += lax.dot_general(
-                tc[1, j], wdn[span(t, ft), pl.ds(j * col, col)], contract_last, preferred_element_type=f32
-            )
-        scaled = weight * back
-        gp_own[t, 0] = (scaled * fac_buf[t]).astype(bf16)
-        gp_own[t, 1] = (scaled * act_buf[t]).astype(bf16)
-        route = route + jnp.sum(hid_buf[t].astype(f32) * back, axis=1, keepdims=True)
-        for r in (1, 0):
-            h_copy(1, r, t).start()
-        return route
-
-    route = lax.fori_loop(0, tiles, back_step, jnp.zeros((rows, 1), f32))
-    for d in range(2, nz):
-        pass_on(2, d)
-    lined = jnp.broadcast_to(route, (rows, 128)).T
-    for p in range(ep_size):
-        line = lined[0:1, p * count:(p + 1) * count]
-        rs[p, :, 0:count] = jnp.broadcast_to(line, (rs.shape[1], count))
-
-    def slot_step(n, carry):
-        total = jnp.zeros((rows, col), f32)
-        for t in range(tiles):
-            lanes = pl.ds(t * ft, ft)
-            total += lax.dot_general(gp_own[t, 0], wg[span(n, col), lanes], contract_last, preferred_element_type=f32)
-            total += lax.dot_general(gp_own[t, 1], wu[span(n, col), lanes], contract_last, preferred_element_type=f32)
-        part[n] = total.reshape(2, half, col)
-        ys[n] = part[n, 1 - y].astype(bf16)
-        remote(ys.at[n], yr.at[n], y_send.at[n], y_recv.at[n], ynb, dp).start()
-        return carry
-
-    lax.fori_loop(0, groups, slot_step, 0)
+        ref = cols.at[1, r, span(ep, count)]
+        remote(ref, ref, c_send.at[1, r], c_recv.at[1, r], ep, peers_dp[r]).wait_recv()
+    own_out(2)
+    slot_step(0, inner)
+    outer_pass(0, near)
+    outer_pass(0, far)
+    take(0, near_o)
+    take(0, far_o)
+    outer_pass(1, near)
+    gate_step(1)
+    outer_pass(1, far)
+
+    @pl.when(outer)
+    def _():
+        def step(n, carry):
+            y_copy(0, n).start()
+            return carry
+
+        lax.fori_loop(0, groups, step, 0)
+
+    pass_hidden(0)
+    pair_out(2)
+    take(1, near_o)
+    take(1, far_o)
+    back_step(1)
+    inner_pass(2, near)
+    inner_pass(2, far)
+    slot_step(1, None)
+    pass_grad_first()
+    y_add(0)
+    outer_pass(2, near)
+    outer_pass(2, far)
     for k in range(1, ep_size):
         to = (ep + k) % ep_size
-        pos = (to % 2) * nz + to // 2
-        remote(rs.at[pos], rr.at[ep], r_send.at[k], r_recv.at[ep], to, dp).start()
-    rr[ep] = rs[mine]
-    for t in range(tiles):
-        forward(0, t)
-
-    def add_step(n, carry):
-        remote(ys.at[n], yr.at[n], y_send.at[n], y_recv.at[n], ynb, dp).wait()
-        total = part[n, y] + yr[n].astype(f32)
-        part[n, y] = total
-        zs[n] = total.astype(bf16)
-        for k in range(1, nz):
-            to = (z + k) % nz
-            remote(
-                zs.at[n, span(to, count)], zr.at[n, k - 1], z_send.at[n, k - 1], z_recv.at[n, k - 1], to * 2 + y, dp
-            ).start()
-        return carry
-
-    lax.fori_loop(0, groups, add_step, 0)
+        remote(rs.at[to], rr.at[ep], r_sem.at[0], r_sem.at[1], to, dp).start()
+    pltpu.make_async_copy(rs.at[ep], rr.at[ep], r_sem.at[1]).start()
+    pass_hidden(1)
     colst[0] = tc[0, dp].T
     for r in range(3):
         remote(cols.at[0, r], cols.at[0, r], c_send.at[0, r], c_recv.at[0, r], ep, peers_dp[r]).wait_recv()
         colst[1 + r] = cols[0, r].T
+    y_add(1)
+    z_add(0)
     remote(cols.at[1, 0], cols.at[1, 0], c_send.at[1, 0], c_recv.at[1, 0], ep, peers_dp[0]).wait_recv()
-    take_side(2)
-    forward(1, 0)
+    got_diag(2)
+    got(2, near_o)
+    got(2, far_o)
+    remote(hw_recv.at[0], hw_recv.at[0], h_send.at[0, 0], h_done.at[0], ep, peers_dp[0]).wait_recv()
+    remote(hw_recv.at[2], hw_recv.at[2], h_send.at[0, 2], h_done.at[3], ep, peers_dp[0]).wait_recv()
 
     def down_step(t, carry):
-        for r in (0, 2):
-            h_copy(0, r, t).wait_recv()
         blocks = [hw_own.at[t]] + [hw_recv.at[r, t] for r in range(3)]
         cots = [tc.at[1, dp]] + [cols.at[1, r] for r in range(3)]
         grad_down = jnp.zeros((ft, col), f32)
@@ -422,28 +541,28 @@
         return carry
 
     lax.fori_loop(0, tiles, down_step, 0)
+    z_add(1)
+    remote(gp_recv.at[0], gp_recv.at[0], h_send.at[1, 0], h_done.at[4], ep, peers_dp[0]).wait_recv()
+    ref = gp_recv.at[2, :, :, wave_rows(0)]
+    remote(ref, ref, h_send.at[1, 2], h_done.at[6 + tiles], ep, peers_dp[0]).wait_recv()
+    pass_grad(0)
 
     def sum_step(n, carry):
-        total = part[n, y, span(z, count), :]
-        for k in range(1, nz):
-            remote(
-                zs.at[n, pl.ds(0, count)], zr.at[n, k - 1], z_send.at[n, k - 1], z_recv.at[n, k - 1], ep, dp
-            ).wait()
-            total = total + zr[n, k - 1].astype(f32)
-        gt_ref[:, span(n, col)] = total.astype(bf16)
+        remote(xs.at[n], xr.at[n], x_sem.at[0], x_sem.at[1 + n], twin, dp).wait_recv()
+        gt_ref[:, span(n, col)] = (part[0, n, i, y] + xr[n].astype(f32)).astype(bf16)
         return carry
 
     def weight_step(t, carry):
         @pl.when(t + 1 < tiles)
         def _():
-            forward(1, t + 1)
+            pass_grad(t + 1)
 
         @pl.when(t + 1 == tiles)
         def _():
             lax.fori_loop(0, groups, sum_step, 0)
 
-        for r in (0, 2):
-            h_copy(1, r, t).wait_recv()
+        ref = gp_recv.at[2, t, :, wave_rows(1)]
+        remote(ref, ref, h_send.at[1, 2], h_done.at[7 + tiles + t], ep, peers_dp[0]).wait_recv()
         blocks = [gp_own.at[t]] + [gp_recv.at[r, t] for r in range(3)]
         grad_gate = jnp.zeros((col, ft), f32)
         grad_up = jnp.zeros((col, ft), f32)
@@ -456,33 +575,38 @@
 
     lax.fori_loop(0, tiles, weight_step, 0)
 
-    for k in range(1, ep_size):
-        frm = (ep + k) % ep_size
-        remote(rs.at[0], rr.at[frm], r_send.at[k], r_recv.at[frm], ep, dp).wait()
-        remote(wd.at[0], wbuf.at[mine], w_send.at[k], w_recv.at[mine], ep, dp).wait_send()
+    remote(rr, rr, r_sem.at[0], r_sem.at[1], ynb, dp).wait_recv()
     table = jnp.zeros(ids.shape, f32)
     for e in range(ep_size):
         table = table + jnp.where(ids == e, rr[e, 0:1, 0:count], 0.0)
     route_ref[...] = table.astype(bf16)
-    for which in range(3):
-        for zz in range(nz):
-            block_copy(which, 2, zz, ep).wait_send()
-
-            @pl.when(jnp.logical_and(z >= zz, z + 1 < nz))
-            def _():
-                block_copy(which, 0, zz, ep).wait_send()
-
-            @pl.when(jnp.logical_and(z <= zz, z > 0))
-            def _():
-                block_copy(which, 1, zz, ep).wait_send()
-
-    for which in range(2):
+
+    def sent(ref, sem):
+        remote(ref, ref, sem, r_sem.at[1], ynb, dp).wait_send()
+
+    sent(rs.at[pl.ds(0, ep_size - 1)], r_sem.at[0])
+    sent(wd.at[pl.ds(0, ep_size - 1)], w_sem.at[0])
+    sent(ys, y_sem.at[0])
+    sent(zs, z_sem.at[0])
+    sent(xs, x_sem.at[0])
+    for k in range(3):
+        def whole(n):
+            return cols.at[1, pl.ds(1, 2), pl.ds(0, n * count)] if k == 2 else tc.at[k, :, pl.ds(0, n * count)]
+
+        sent(whole(3), g_send.at[k, 0])
+
+        @pl.when(inner)
+        def _():
+            sent(whole(6), g_send.at[k, 1])
+
+        @pl.when(outer)
+        def _():
+            sent(whole(2), g_send.at[k, 1])
+
+    for k in range(2):
         for r in range(3):
-            view = cols.at[1, r, span(mine, count)] if which == 1 and r > 0 else cols.at[which, r]
-            remote(view, view, c_send.at[which, r], c_recv.at[which, r], ep, peers_dp[r]).wait_send()
-        for t in range(tiles):
-            for r in range(3):
-                h_copy(which, r, t).wait_send()
+            sent(cols.at[1, r, pl.ds(0, count)] if k == 1 and r > 0 else cols.at[k, r], c_send.at[k, r])
+            sent((hw_recv, gp_recv)[k].at[r], h_send.at[k, r])
 
 
 def store_kernel(*refs):
@@ -512,7 +636,6 @@
     hbm = pl.BlockSpec(memory_space=pltpu.HBM)
     vmem = pl.BlockSpec(memory_space=pltpu.VMEM)
     dma = pltpu.SemaphoreType.DMA
-    nz = experts // 2
     small = (experts, 8, lanes)
     shapes = ((count, model), (topk, count), (col, width), (col, width), (width, col))
     outs = pl.pallas_call(
@@ -530,6 +653,7 @@
             pltpu.VMEM((2, groups, rows, col), bf16),
             pltpu.VMEM(small, f32),
             pltpu.VMEM(small, f32),
+            pltpu.VMEM((rows, lanes), f32),
             pltpu.VMEM((2, 3, rows, col), bf16),
             pltpu.VMEM((4, col, rows), bf16),
             pltpu.VMEM((tiles, rows, ft), f32),
@@ -539,28 +663,27 @@
             pltpu.VMEM((3, tiles, rows, ft), bf16),
             pltpu.VMEM((tiles, 2, rows, ft), bf16),
             pltpu.VMEM((3, tiles, 2, rows, ft), bf16),
-            pltpu.VMEM((groups, 2, rows // 2, col), f32),
-            pltpu.VMEM((groups, rows // 2, col), bf16),
-            pltpu.VMEM((groups, rows // 2, col), bf16),
-            pltpu.VMEM((groups, rows // 2, col), bf16),
-            pltpu.VMEM((groups, nz - 1, count, col), bf16),
+            pltpu.VMEM((2, groups, 2, 2, count, col), f32),
+            pltpu.VMEM((2, groups, 2, count, col), bf16),
+            pltpu.VMEM((2, groups, 2, count, col), bf16),
+            pltpu.VMEM((2, groups, count, col), bf16),
+            pltpu.VMEM((2, groups, count, col), bf16),
+            pltpu.VMEM((groups, count, col), bf16),
+            pltpu.VMEM((groups, count, col), bf16),
             pltpu.VMEM(small, f32),
             pltpu.VMEM(small, f32),
-            dma((4, max(groups, 4))),
-            dma((experts,)),
-            dma((experts,)),
-            dma((3, 3, nz)),
+            dma((7,)),
+            dma((2,)),
+            dma((3, 2)),
             dma((3, experts)),
             dma((2, 3)),
             dma((2, 3)),
-            dma((2, 3, tiles)),
-            dma((2, 3, tiles)),
-            dma((groups,)),
-            dma((groups,)),
-            dma((groups, nz - 1)),
-            dma((groups, nz - 1)),
-            dma((experts,)),
-            dma((experts,)),
+            dma((2, 3)),
+            dma((7 + 2 * tiles,)),
+            dma((2 + groups,)),
+            dma((2 + groups,)),
+            dma((1 + groups,)),
+            dma((2,)),
         ],
         compiler_params=pltpu.CompilerParams(
             collective_id=0, has_side_effects=True, vmem_limit_bytes=64200000
@@ -583,7 +706,7 @@
     tok_count, topk = expert_ids.shape
     experts = lax.axis_size("ep")
     whole = 2 * tok_count * topk // experts >= tok_count
-    paired = lax.axis_size("dp") == 4 and experts in (4, 8, 16) and tok_count in (16, 32, 64, 128)
+    paired = lax.axis_size("dp") == 4 and experts == 8 and tok_count in (32, 64)
     chosen = fused_body if whole and paired else routed_body
     return chosen(tokens, cotangent, expert_ids, route_weights, w_gate, w_up, w_down)
 

time: 60.8 us -> 60.2 us (level)
    pallas_call x1, Pallas kernels: 58.5 us -> 57.8 us  [fused_body(): pl.pallas_call(fused_kernel, name='fused_layer', out_shape=tuple((pltpu.V...]
where the time goes in v1:
time: 60.2 us; the launch traced here: 60 us
  Pallas kernels  59.3 us (99%)
  between operations  0.64 us (1%)
    pallas_call x1, Pallas kernels, fused_body(): pl.pallas_call(fused_kernel, name='fused_layer', out_shape=tuple((pltpu.V...  57.8 us
    pallas_call x1, Pallas kernels, fused_body(): pl.pallas_call(store_kernel, name='store_results', out_shape=tuple((jax.S...  1.49 us

profile of v1, /device:TPU:0, one launch (start us, length us, event | category | flops | bytes accessed | tf_op | source)
XLA Modules:
  0.0 60.0 jit_solution(3772887098531209429)
XLA Ops:
  0.6 57.8 %fused_layer.1 = (bf16[32,2048]{1,0:T(8,128)(2,1)S(1)}, bf16[8,32]{1,0:T(8,128)(2,1)S(1)}, bf16[512,768]{1,0:T(8,128)(2,1)S(1)}, bf16[512,768]{1,0:T(8,128)(2,1)S(1)}, bf16[768,512]{1,0:T(8,128)(2,1)S(1)}) custom-call(bf16[32,2048]{1,0:T(8,128)(2,1)} %tok_hbm.1, bf16[32,2048]{1,0:T(8,128)(2,1)} %cot_hbm.1, s32[8,32]{1,0:T(8,128)} %bitcast.12, ...), custom_call_target="tpu_custom_call" | custom-call | tf_op jit(solution)/shard_map/fused_layer/pallas_call | solution.py:641
  58.5 1.5 %store_results.1 = (bf16[32,2048]{1,0:T(8,128)(2,1)}, bf16[8,32]{1,0:T(8,128)(2,1)}, bf16[512,768]{1,0:T(8,128)(2,1)}, bf16[512,768]{1,0:T(8,128)(2,1)}, bf16[768,512]{1,0:T(8,128)(2,1)}) custom-call(bf16[32,2048]{1,0:T(8,128)(2,1)S(1)} %get-tuple-element.15.refs_0_, bf16[8,32]{1,0:T(8,128)(2,1)S(1)} %get-tuple-element.16.refs_1_, ...), custom_call_target="tpu_custom_call" | custom-call | tf_op jit(solution)/shard_map/store_results/pallas_call | solution.py:692

commit v2 on v1

--- a/solution.py
+++ b/solution.py
@@ -6,6 +6,7 @@
 from jax.sharding import PartitionSpec as P
 
 block_rows = 128
+lead = 3
 contract_last = (((1,), (1,)), ((), ()))
 contract_first = (((0,), (0,)), ((), ()))
 
@@ -158,15 +159,14 @@
     tok_hbm, cot_hbm, ids_hbm, rw_hbm, wg_hbm, wu_hbm, wdn_hbm,
     gt_ref, route_ref, gg_ref, gu_ref, gd_ref,
     ids_ref, rw_ref, wg, wu, wdn, tc, wd, wbuf, wcol, cols, colst, act_buf, fac_buf, hid_buf,
-    hw_own, hw_recv, gp_own, gp_recv, part, ys, yr, zs, zr, xs, xr, rs, rr,
-    l_sem, w_sem, g_send, g_recv, c_send, c_recv, h_send, h_done, y_sem, z_sem, x_sem, r_sem,
+    hw_own, hw_recv, gp_own, gp_recv, part, fs, fr, bs, br, xs, xr, rs, rr,
+    l_sem, w_sem, g_send, g_recv, c_send, c_recv, h_send, h_done, f_sem, b_sem, x_sem, r_sem,
 ):
     ep_size = lax.axis_size("ep")
     groups = lax.axis_size("dp")
     count = tok_hbm.shape[0]
     col = tc.shape[3]
     tiles, rows, ft = hw_own.shape
-    half = rows // 2
     ep = lax.axis_index("ep")
     dp = lax.axis_index("dp")
     z, y = ep // 2, ep % 2
@@ -175,19 +175,17 @@
     peers_dp = (xx * 2 + 1 - core, (1 - xx) * 2 + core, (1 - xx) * 2 + 1 - core)
     inner = i != q
     outer = i == q
-    zp = z + 1 - 2 * i
-    ynb = z * 2 + 1 - y
-    znb = zp * 2 + y
-    diag = zp * 2 + 1 - y
-    near = (2 - q) * 2 + y
-    far = (3 - 3 * q) * 2 + y
-    near_o = (2 - q) * 2 + 1 - y
-    far_o = (3 - 3 * q) * 2 + 1 - y
-    twin = (ep + 4) % 8
-    pairs = (q, 1 - q)
+    zline = (z, z + 1 - 2 * i, z + 2 - 4 * q, 3 - z)
+    targets = tuple(zline[s // 2] * 2 + (1 - y if s % 2 else y) for s in range(8))
+    ynb, znb, twin, facing = targets[1], targets[2], targets[4], targets[6]
+    inside = (i + q) % 2
+    near = 4 + 2 * inside
+    far = 6 - 2 * inside
+    starts = (0, lead)
+    sizes = (lead, 8 - lead)
+    early = lead - 2
     f32 = jnp.float32
     bf16 = jnp.bfloat16
-    first = 1
 
     def span(index, size):
         return pl.ds(pl.multiple_of(index * size, size), size)
@@ -200,7 +198,7 @@
 
     loads = [
         [
-            pltpu.make_async_copy(ref.at[:, pl.ds(j * col, col)], tc.at[k, j, span(ep, count)], l_sem.at[k])
+            pltpu.make_async_copy(ref.at[:, pl.ds(j * col, col)], tc.at[k, j, pl.ds(0, count)], l_sem.at[k])
             for j in range(groups)
         ]
         for k, ref in enumerate((tok_hbm, cot_hbm))
@@ -219,6 +217,8 @@
         for k, (src, dst) in enumerate(((wg_hbm, wg), (wu_hbm, wu), (wdn_hbm, wdn)))
     ]
 
+    for load in w_loads:
+        load.start()
     barrier = pltpu.get_barrier_semaphore()
     for k in range(1, ep_size):
         pl.semaphore_signal(
@@ -237,98 +237,83 @@
         wd[e, :, 0:count] = jnp.broadcast_to(line, (wd.shape[1], count))
     pl.semaphore_wait(barrier, ep_size - 1 + len(peers_dp))
 
-    def view(k, pos, piece):
+    def view(k, slot):
+        place = span(slot, count)
+        return cols.at[1, pl.ds(1, 2), place] if k == 2 else tc.at[k, :, place]
+
+    def hop(k, slot, there, late, ep_to):
+        remote(view(k, slot), view(k, there), g_send.at[k, late], g_recv.at[k, there], ep_to, dp).start()
+
+    def got(k, slot):
+        remote(view(k, slot), view(k, slot), g_send.at[k, 0], g_recv.at[k, slot], ynb, dp).wait_recv()
+
+    def share(k, slot, every=False):
         if k == 2:
-            return cols.at[1, pl.ds((1, 1, 2)[piece], (2, 1, 1)[piece]), span(pos, count)]
-        return tc.at[k, pl.ds((0, 0, first)[piece], (groups, first, groups - first)[piece]), span(pos, count)]
-
-    def hop(k, pos, piece, late, ep_to):
-        ref = view(k, pos, piece)
-        slot = ep_to if piece == 2 else pos
-        remote(ref, ref, g_send.at[k, late], g_recv.at[k, slot], ep_to, dp).start()
-
-    def got(k, pos):
-        ref = view(k, pos, 0)
-        remote(ref, ref, g_send.at[k, 0], g_recv.at[k, pos], ynb, dp).wait_recv()
-
-    def got_diag(k):
-        ref = view(k, diag, 1)
-        remote(ref, ref, g_send.at[k, 0], g_recv.at[k, diag], ynb, dp).wait_recv()
-        ref = view(k, diag, 2)
-        remote(ref, ref, g_send.at[k, 0], g_recv.at[k, ep], znb, dp).wait_recv()
-
-    def send_cols(k, pos, reach):
-        for r in (1, 2, 0)[3 - reach:] if reach == 3 else (0,):
+            return
+        for r in (1, 2, 0) if k == 0 or every else (0,):
             peer = peers_dp[r]
             remote(
-                tc.at[k, peer, span(pos, count)], cols.at[k, r, span(pos, count)],
+                tc.at[k, peer, span(slot, count)], cols.at[k, r, span(slot, count)],
                 c_send.at[k, r], c_recv.at[k, r], ep, peer,
             ).start()
 
-    def share(k, pos):
-        if k < 2:
-            send_cols(k, pos, 3 - 2 * k)
+    def take(k, slot):
+        got(k, slot)
+        share(k, slot)
 
     def own_out(k):
-        hop(k, ep, 0, 0, ynb)
-        hop(k, ep, 0, 0, znb)
+        hop(k, 0, 1, 0, ynb)
+        hop(k, 0, 2, 0, znb)
 
         @pl.when(inner)
         def _():
-            hop(k, ep, 0, 1, near)
+            hop(k, 0, 6, 1, facing)
 
     def pair_out(k):
-        got(k, znb)
-        hop(k, znb, 1, 0, ynb)
+        got(k, 2)
+        if k < 2:
+            hop(k, 2, 3, 0, ynb)
 
         @pl.when(inner)
         def _():
-            hop(k, znb, 0, 1, near)
-
-        share(k, znb)
-        got(k, ynb)
-        hop(k, ynb, 2, 0, znb)
-        share(k, ynb)
-
-    def inner_pass(k, pos):
+            hop(k, 2, 4, 1, facing)
+
+        share(k, 2)
+        got(k, 1)
+        if k == 2:
+            hop(k, 1, 3, 0, znb)
+        share(k, 1)
+
+    def inner_pass(k, slot):
         @pl.when(inner)
         def _():
-            got(k, pos)
-            hop(k, pos, 0, 1, znb)
-            hop(k, pos, 0, 1, ynb)
-            share(k, pos)
-
-    def outer_pass(k, pos):
+            got(k, slot)
+            hop(k, slot, 10 - slot, 1, znb)
+            hop(k, slot, slot + 1, 1, ynb)
+            share(k, slot)
+
+    def outer_pass(k, slot):
         @pl.when(outer)
         def _():
-            got(k, pos)
-            hop(k, pos, 0, 1, ynb)
-            share(k, pos)
-
-    def take(k, pos):
-        got(k, pos)
-        share(k, pos)
-
+            got(k, slot)
+            hop(k, slot, slot + 1, 1, ynb)
+            share(k, slot)
+
+    for s in range(1, 8):
+        remote(wd.at[targets[s]], wbuf.at[s], w_sem.at[0], w_sem.at[1], targets[s], dp).start()
+    keep_w = pltpu.make_async_copy(wd.at[ep], wbuf.at[0], w_sem.at[1])
+    keep_w.start()
     for k in range(2):
-        ref = view(k, ep, 0)
-        pltpu.make_async_copy(ref, ref, l_sem.at[k]).wait()
+        pltpu.make_async_copy(view(k, 0), view(k, 0), l_sem.at[k]).wait()
         own_out(k)
-        send_cols(k, ep, 3)
-    for k in range(1, ep_size):
-        to = (ep + k) % ep_size
-        remote(wd.at[to], wbuf.at[ep], w_sem.at[0], w_sem.at[1], to, dp).start()
-    keep_w = pltpu.make_async_copy(wd.at[ep], wbuf.at[ep], w_sem.at[1])
-    keep_w.start()
-    for load in w_loads:
-        load.start()
-    pair_out(0)
-    pair_out(1)
+        share(k, 0, True)
 
     def wave_rows(wave):
-        return span(pairs[wave], half)
+        return pl.ds(starts[wave] * count, sizes[wave] * count)
 
     def gate_step(wave):
         block = wave_rows(wave)
+        half = sizes[wave] * count
 
         def step(t, carry):
             lanes = span(t, ft)
@@ -357,6 +342,7 @@
     def back_step(wave):
         block = wave_rows(wave)
         weight = wcol[block, 0:1]
+        half = sizes[wave] * count
 
         def step(t, route):
             back = jnp.zeros((half, ft), f32)
@@ -377,19 +363,27 @@
 
         route = lax.fori_loop(0, tiles, step, jnp.zeros((half, 1), f32))
         lined = jnp.broadcast_to(route, (half, 128)).T
-        for p in range(4):
+        for p in range(sizes[wave]):
             line = lined[0:1, p * count:(p + 1) * count]
-            rs[pairs[wave] * 4 + p, :, 0:count] = jnp.broadcast_to(line, (rs.shape[1], count))
-
-    def y_copy(wave, n):
-        done = y_sem.at[1 + wave * (1 + n)]
-        return remote(ys.at[wave, n], yr.at[wave, n], y_sem.at[0], done, ynb, dp)
-
-    def slot_step(wave, sending):
+            rs[starts[wave] + p, :, 0:count] = jnp.broadcast_to(line, (rs.shape[1], count))
+
+    def fold_send(n, mode, phase):
+        place = pl.ds(early * phase, early + (4 - 2 * early) * phase)
+        done = f_sem.at[1 + phase * (1 + n)]
+        to = ynb + mode * (znb - ynb)
+        return remote(fs.at[n, place], fr.at[n, place], f_sem.at[0], done, to, dp)
+
+    def fold_rows(n, mode, phase):
+        for j in ((range(early), range(early, 4))[phase]):
+            source = 2 * j + 1 + mode * (1 - j % 2)
+            fs[n, j] = part[n, source].astype(bf16)
+
+    def slot_step(wave):
         block = wave_rows(wave)
+        size = sizes[wave]
 
         def step(n, carry):
-            total = jnp.zeros((half, col), f32)
+            total = jnp.zeros((size * count, col), f32)
             for t in range(tiles):
                 lanes = pl.ds(t * ft, ft)
                 total += lax.dot_general(
@@ -398,48 +392,42 @@
                 total += lax.dot_general(
                     gp_own[t, 1, block], wu[span(n, col), lanes], contract_last, preferred_element_type=f32
                 )
-            part[wave, n] = total.reshape(2, 2, count, col)
-            ys[wave, n] = part[wave, n, :, 1 - y].astype(bf16)
-            if sending is None:
-                y_copy(wave, n).start()
-            else:
-                @pl.when(sending)
-                def _():
-                    y_copy(wave, n).start()
+            part[n, pl.ds(starts[wave], size)] = total.reshape(size, count, col)
+            mode = n // 2
+            fold_rows(n, mode, wave)
+            if wave == 1:
+                fold_send(n, mode, 1).start()
             return carry
 
         lax.fori_loop(0, groups, step, 0)
 
-    def y_add(wave):
-        if wave == 0:
-            remote(ys.at[0], yr.at[0], y_sem.at[0], y_sem.at[1], ynb, dp).wait_recv()
-
+    def fold_early():
         def step(n, carry):
-            if wave == 1:
-                y_copy(1, n).wait_recv()
-            total = part[wave, n, :, y] + yr[wave, n].astype(f32)
-            part[wave, n, :, y] = total
-            zs[wave, n] = part[wave, n, 1 - i, y].astype(bf16)
-            remote(
-                zs.at[wave, n], zr.at[wave, n], z_sem.at[0], z_sem.at[1 + wave * (1 + n)], znb, dp
-            ).start()
+            fold_send(n, n // 2, 0).start()
             return carry
 
         lax.fori_loop(0, groups, step, 0)
 
-    def z_add(wave):
-        if wave == 0:
-            remote(zs.at[0], zr.at[0], z_sem.at[0], z_sem.at[1], znb, dp).wait_recv()
+    def fold_mid():
+        ref = fr.at[:, pl.ds(0, early)]
+        remote(ref, ref, f_sem.at[0], f_sem.at[1], ynb, dp).wait_recv()
 
         def step(n, carry):
-            if wave == 1:
-                remote(zs.at[1, n], zr.at[1, n], z_sem.at[0], z_sem.at[2 + n], znb, dp).wait_recv()
-            total = part[wave, n, i, y] + zr[wave, n].astype(f32)
-            if wave == 0:
-                part[0, n, i, y] = total
-            else:
-                xs[n] = total.astype(bf16)
-                remote(xs.at[n], xr.at[n], x_sem.at[0], x_sem.at[1 + n], twin, dp).start()
+            mode = n // 2
+            fold_send(n, mode, 1).wait_recv()
+            bs[n, 0] = (part[n, 2 - mode] + fr[n, 1].astype(f32)).astype(bf16)
+            bs[n, 1] = (part[n, 6 - mode] + fr[n, 3].astype(f32)).astype(bf16)
+            to = znb + mode * (ynb - znb)
+            remote(bs.at[n], br.at[n], b_sem.at[0], b_sem.at[1 + n], to, dp).start()
+            return carry
+
+        lax.fori_loop(0, groups, step, 0)
+
+    def fold_cross():
+        def step(n, carry):
+            remote(bs.at[n], br.at[n], b_sem.at[0], b_sem.at[1 + n], znb, dp).wait_recv()
+            xs[n] = (part[n, 4] + fr[n, 2].astype(f32) + br[n, 1].astype(f32)).astype(bf16)
+            remote(xs.at[n], xr.at[n], x_sem.at[0], x_sem.at[1 + n], twin, dp).start()
             return carry
 
         lax.fori_loop(0, groups, step, 0)
@@ -462,9 +450,10 @@
             ref, gp_recv.at[2, t, :, wave_rows(1)], h_send.at[1, 2], h_done.at[7 + tiles + t], ep, peers_dp[0]
         ).start()
 
-    got_diag(0)
-    share(0, diag)
-    for load in w_loads:
+    pair_out(0)
+    if lead == 4:
+        take(0, 3)
+    for load in w_loads[0:2]:
         load.wait()
     remote(wbuf, wbuf, w_sem.at[0], w_sem.at[1], ynb, dp).wait_recv()
     flat = wbuf[...].reshape(ep_size * wbuf.shape[1], wbuf.shape[2])
@@ -474,60 +463,56 @@
         wcol[pl.ds(p * count, count), :] = jnp.broadcast_to(turned[0:count, p * step8:p * step8 + 1], (count, 128))
     gate_step(0)
     inner_pass(0, near)
+    pair_out(1)
+    if lead == 4:
+        take(1, 3)
+    w_loads[2].wait()
+    back_step(0)
     inner_pass(0, far)
-    inner_pass(1, near)
-    got_diag(1)
-    share(1, diag)
-    back_step(0)
-    inner_pass(1, far)
     for r in (1, 2):
-        ref = cols.at[1, r, span(ep, count)]
+        ref = cols.at[1, r, pl.ds(0, count)]
         remote(ref, ref, c_send.at[1, r], c_recv.at[1, r], ep, peers_dp[r]).wait_recv()
     own_out(2)
-    slot_step(0, inner)
+    slot_step(0)
+    inner_pass(1, near)
+    inner_pass(1, far)
     outer_pass(0, near)
     outer_pass(0, far)
-    take(0, near_o)
-    take(0, far_o)
+    if lead == 3:
+        take(0, 3)
+    take(0, near + 1)
     outer_pass(1, near)
+    take(0, far + 1)
     gate_step(1)
     outer_pass(1, far)
-
-    @pl.when(outer)
-    def _():
-        def step(n, carry):
-            y_copy(0, n).start()
-            return carry
-
-        lax.fori_loop(0, groups, step, 0)
-
+    fold_early()
+    pair_out(2)
     pass_hidden(0)
-    pair_out(2)
-    take(1, near_o)
-    take(1, far_o)
+    if lead == 3:
+        take(1, 3)
+    take(1, near + 1)
+    take(1, far + 1)
     back_step(1)
     inner_pass(2, near)
+    slot_step(1)
+    pass_grad_first()
+    for s in range(1, 8):
+        remote(rs.at[s], rr.at[ep], r_sem.at[0], r_sem.at[1], targets[s], dp).start()
+    pltpu.make_async_copy(rs.at[0], rr.at[ep], r_sem.at[1]).start()
     inner_pass(2, far)
-    slot_step(1, None)
-    pass_grad_first()
-    y_add(0)
-    outer_pass(2, near)
-    outer_pass(2, far)
-    for k in range(1, ep_size):
-        to = (ep + k) % ep_size
-        remote(rs.at[to], rr.at[ep], r_sem.at[0], r_sem.at[1], to, dp).start()
-    pltpu.make_async_copy(rs.at[ep], rr.at[ep], r_sem.at[1]).start()
     pass_hidden(1)
     colst[0] = tc[0, dp].T
     for r in range(3):
         remote(cols.at[0, r], cols.at[0, r], c_send.at[0, r], c_recv.at[0, r], ep, peers_dp[r]).wait_recv()
         colst[1 + r] = cols[0, r].T
-    y_add(1)
-    z_add(0)
+    fold_mid()
+    outer_pass(2, near)
+    outer_pass(2, far)
     remote(cols.at[1, 0], cols.at[1, 0], c_send.at[1, 0], c_recv.at[1, 0], ep, peers_dp[0]).wait_recv()
-    got_diag(2)
-    got(2, near_o)
-    got(2, far_o)
+    fold_cross()
+    got(2, 3)
+    got(2, near + 1)
+    got(2, far + 1)
     remote(hw_recv.at[0], hw_recv.at[0], h_send.at[0, 0], h_done.at[0], ep, peers_dp[0]).wait_recv()
     remote(hw_recv.at[2], hw_recv.at[2], h_send.at[0, 2], h_done.at[3], ep, peers_dp[0]).wait_recv()
 
@@ -541,7 +526,6 @@
         return carry
 
     lax.fori_loop(0, tiles, down_step, 0)
-    z_add(1)
     remote(gp_recv.at[0], gp_recv.at[0], h_send.at[1, 0], h_done.at[4], ep, peers_dp[0]).wait_recv()
     ref = gp_recv.at[2, :, :, wave_rows(0)]
     remote(ref, ref, h_send.at[1, 2], h_done.at[6 + tiles], ep, peers_dp[0]).wait_recv()
@@ -549,7 +533,8 @@
 
     def sum_step(n, carry):
         remote(xs.at[n], xr.at[n], x_sem.at[0], x_sem.at[1 + n], twin, dp).wait_recv()
-        gt_ref[:, span(n, col)] = (part[0, n, i, y] + xr[n].astype(f32)).astype(bf16)
+        total = part[n, 0] + fr[n, 0].astype(f32) + br[n, 0].astype(f32) + xr[n].astype(f32)
+        gt_ref[:, span(n, col)] = total.astype(bf16)
         return carry
 
     def weight_step(t, carry):
@@ -586,8 +571,8 @@
 
     sent(rs.at[pl.ds(0, ep_size - 1)], r_sem.at[0])
     sent(wd.at[pl.ds(0, ep_size - 1)], w_sem.at[0])
-    sent(ys, y_sem.at[0])
-    sent(zs, z_sem.at[0])
+    sent(fs, f_sem.at[0])
+    sent(bs, b_sem.at[0])
     sent(xs, x_sem.at[0])
     for k in range(3):
         def whole(n):
@@ -663,11 +648,11 @@
             pltpu.VMEM((3, tiles, rows, ft), bf16),
             pltpu.VMEM((tiles, 2, rows, ft), bf16),
             pltpu.VMEM((3, tiles, 2, rows, ft), bf16),
-            pltpu.VMEM((2, groups, 2, 2, count, col), f32),
-            pltpu.VMEM((2, groups, 2, count, col), bf16),
-            pltpu.VMEM((2, groups, 2, count, col), bf16),
-            pltpu.VMEM((2, groups, count, col), bf16),
-            pltpu.VMEM((2, groups, count, col), bf16),
+            pltpu.VMEM((groups, 8, count, col), f32),
+            pltpu.VMEM((groups, 4, count, col), bf16),
+            pltpu.VMEM((groups, 4, count, col), bf16),
+            pltpu.VMEM((groups, 2, count, col), bf16),
+            pltpu.VMEM((groups, 2, count, col), bf16),
             pltpu.VMEM((groups, count, col), bf16),
             pltpu.VMEM((groups, count, col), bf16),
             pltpu.VMEM(small, f32),
@@ -681,7 +666,7 @@
             dma((2, 3)),
             dma((7 + 2 * tiles,)),
             dma((2 + groups,)),
-            dma((2 + groups,)),
+            dma((1 + groups,)),
             dma((1 + groups,)),
             dma((2,)),
         ],

time: 60.2 us -> 56.8 us (0.944)
  Pallas kernels: 59.3 us -> 56.1 us
    pallas_call x1, Pallas kernels: 57.8 us -> 54.6 us  [fused_body(): pl.pallas_call(fused_kernel, name='fused_layer', out_shape=tuple((pltpu.V...]
where the time goes in v2:
time: 56.8 us; the launch traced here: 56.7 us
  Pallas kernels  56.1 us (99%)
  between operations  0.64 us (1%)
    pallas_call x1, Pallas kernels, fused_body(): pl.pallas_call(fused_kernel, name='fused_layer', out_shape=tuple((pltpu.V...  54.6 us
    pallas_call x1, Pallas kernels, fused_body(): pl.pallas_call(store_kernel, name='store_results', out_shape=tuple((jax.S...  1.49 us

profile of v2, /device:TPU:0, one launch (start us, length us, event | category | flops | bytes accessed | tf_op | source)
XLA Modules:
  0.0 56.7 jit_solution(2808623889752413473)
XLA Ops:
  0.6 54.6 %fused_layer.1 = (bf16[32,2048]{1,0:T(8,128)(2,1)S(1)}, bf16[8,32]{1,0:T(8,128)(2,1)S(1)}, bf16[512,768]{1,0:T(8,128)(2,1)S(1)}, bf16[512,768]{1,0:T(8,128)(2,1)S(1)}, bf16[768,512]{1,0:T(8,128)(2,1)S(1)}) custom-call(bf16[32,2048]{1,0:T(8,128)(2,1)} %tok_hbm.1, bf16[32,2048]{1,0:T(8,128)(2,1)} %cot_hbm.1, s32[8,32]{1,0:T(8,128)} %bitcast.12, ...), custom_call_target="tpu_custom_call" | custom-call | tf_op jit(solution)/shard_map/fused_layer/pallas_call | solution.py:626
  55.2 1.5 %store_results.1 = (bf16[32,2048]{1,0:T(8,128)(2,1)}, bf16[8,32]{1,0:T(8,128)(2,1)}, bf16[512,768]{1,0:T(8,128)(2,1)}, bf16[512,768]{1,0:T(8,128)(2,1)}, bf16[768,512]{1,0:T(8,128)(2,1)}) custom-call(bf16[32,2048]{1,0:T(8,128)(2,1)S(1)} %get-tuple-element.15.refs_0_, bf16[8,32]{1,0:T(8,128)(2,1)S(1)} %get-tuple-element.16.refs_1_, ...), custom_call_target="tpu_custom_call" | custom-call | tf_op jit(solution)/shard_map/store_results/pallas_call | solution.py:677

commit v3 on v2

--- a/solution.py
+++ b/solution.py
@@ -7,6 +7,8 @@
 
 block_rows = 128
 lead = 3
+store_pieces = 4
+along_y = 2
 contract_last = (((1,), (1,)), ((), ()))
 contract_first = (((0,), (0,)), ((), ()))
 
@@ -158,7 +160,7 @@
 def fused_kernel(
     tok_hbm, cot_hbm, ids_hbm, rw_hbm, wg_hbm, wu_hbm, wdn_hbm,
     gt_ref, route_ref, gg_ref, gu_ref, gd_ref,
-    ids_ref, rw_ref, wg, wu, wdn, tc, wd, wbuf, wcol, cols, colst, act_buf, fac_buf, hid_buf,
+    ids_ref, rw_ref, wg, wu, wdn, wgt, wut, wdt, tc, wd, wbuf, wcol, cols, colst, act_buf, fac_buf, hid_buf,
     hw_own, hw_recv, gp_own, gp_recv, part, fs, fr, bs, br, xs, xr, rs, rr,
     l_sem, w_sem, g_send, g_recv, c_send, c_recv, h_send, h_done, f_sem, b_sem, x_sem, r_sem,
 ):
@@ -166,6 +168,7 @@
     groups = lax.axis_size("dp")
     count = tok_hbm.shape[0]
     col = tc.shape[3]
+    model = wdn.shape[1]
     tiles, rows, ft = hw_own.shape
     ep = lax.axis_index("ep")
     dp = lax.axis_index("dp")
@@ -217,8 +220,8 @@
         for k, (src, dst) in enumerate(((wg_hbm, wg), (wu_hbm, wu), (wdn_hbm, wdn)))
     ]
 
-    for load in w_loads:
-        load.start()
+    for k in (2, 0, 1):
+        w_loads[k].start()
     barrier = pltpu.get_barrier_semaphore()
     for k in range(1, ep_size):
         pl.semaphore_signal(
@@ -242,10 +245,10 @@
         return cols.at[1, pl.ds(1, 2), place] if k == 2 else tc.at[k, :, place]
 
     def hop(k, slot, there, late, ep_to):
-        remote(view(k, slot), view(k, there), g_send.at[k, late], g_recv.at[k, there], ep_to, dp).start()
+        remote(view(k, slot), view(k, there), g_send.at[0], g_recv.at[k, there], ep_to, dp).start()
 
     def got(k, slot):
-        remote(view(k, slot), view(k, slot), g_send.at[k, 0], g_recv.at[k, slot], ynb, dp).wait_recv()
+        remote(view(k, slot), view(k, slot), g_send.at[0], g_recv.at[k, slot], ynb, dp).wait_recv()
 
     def share(k, slot, every=False):
         if k == 2:
@@ -254,7 +257,7 @@
             peer = peers_dp[r]
             remote(
                 tc.at[k, peer, span(slot, count)], cols.at[k, r, span(slot, count)],
-                c_send.at[k, r], c_recv.at[k, r], ep, peer,
+                c_send.at[0], c_recv.at[0 if k == 0 else 1 if r == 0 else 2], ep, peer,
             ).start()
 
     def take(k, slot):
@@ -271,18 +274,28 @@
 
     def pair_out(k):
         got(k, 2)
-        if k < 2:
-            hop(k, 2, 3, 0, ynb)
+        hop(k, 2, 3, 0, ynb)
 
         @pl.when(inner)
         def _():
             hop(k, 2, 4, 1, facing)
 
         share(k, 2)
+        take(k, 1)
+
+    def facing_out(k):
+        @pl.when(inner)
+        def _():
+            got(k, 2)
+            hop(k, 2, 4, 1, facing)
+
+    def diag_out(k):
+        @pl.when(outer)
+        def _():
+            got(k, 2)
+
         got(k, 1)
-        if k == 2:
-            hop(k, 1, 3, 0, znb)
-        share(k, 1)
+        hop(k, 1, 3, 0, znb)
 
     def inner_pass(k, slot):
         @pl.when(inner)
@@ -333,7 +346,7 @@
             for r in (1, 0):
                 done = h_done.at[1 + wave] if r == 1 else h_done.at[0]
                 remote(
-                    hw_own.at[t, block], hw_recv.at[r, t, block], h_send.at[0, r], done, ep, peers_dp[r]
+                    hw_own.at[t, block], hw_recv.at[r, t, block], h_send.at[0], done, ep, peers_dp[r]
                 ).start()
             return carry
 
@@ -347,9 +360,7 @@
         def step(t, route):
             back = jnp.zeros((half, ft), f32)
             for j in range(groups):
-                back += lax.dot_general(
-                    tc[1, j, block], wdn[span(t, ft), pl.ds(j * col, col)], contract_last, preferred_element_type=f32
-                )
+                back += jnp.dot(tc[1, j, block], wdt[pl.ds(j * col, col), span(t, ft)], preferred_element_type=f32)
             scaled = weight * back
             gp_own[t, 0, block] = (scaled * fac_buf[t, block]).astype(bf16)
             gp_own[t, 1, block] = (scaled * act_buf[t, block]).astype(bf16)
@@ -357,7 +368,7 @@
             for r in (1, 0):
                 done = h_done.at[(5 + wave) + wave * t] if r == 1 else h_done.at[4]
                 remote(
-                    gp_own.at[t, :, block], gp_recv.at[r, t, :, block], h_send.at[1, r], done, ep, peers_dp[r]
+                    gp_own.at[t, :, block], gp_recv.at[r, t, :, block], h_send.at[1], done, ep, peers_dp[r]
                 ).start()
             return route
 
@@ -382,18 +393,23 @@
         block = wave_rows(wave)
         size = sizes[wave]
 
-        def step(n, carry):
+        def step(turn, carry):
+            n = turn % 2 * (groups // 2) + turn // 2
             total = jnp.zeros((size * count, col), f32)
             for t in range(tiles):
-                lanes = pl.ds(t * ft, ft)
-                total += lax.dot_general(
-                    gp_own[t, 0, block], wg[span(n, col), lanes], contract_last, preferred_element_type=f32
-                )
-                total += lax.dot_general(
-                    gp_own[t, 1, block], wu[span(n, col), lanes], contract_last, preferred_element_type=f32
-                )
+                depth = pl.ds(t * ft, ft)
+                if wave == 0:
+                    total += lax.dot_general(
+                        gp_own[t, 0, block], wg[span(n, col), depth], contract_last, preferred_element_type=f32
+                    )
+                    total += lax.dot_general(
+                        gp_own[t, 1, block], wu[span(n, col), depth], contract_last, preferred_element_type=f32
+                    )
+                else:
+                    total += jnp.dot(gp_own[t, 0, block], wgt[depth, span(n, col)], preferred_element_type=f32)
+                    total += jnp.dot(gp_own[t, 1, block], wut[depth, span(n, col)], preferred_element_type=f32)
             part[n, pl.ds(starts[wave], size)] = total.reshape(size, count, col)
-            mode = n // 2
+            mode = n // along_y
             fold_rows(n, mode, wave)
             if wave == 1:
                 fold_send(n, mode, 1).start()
@@ -403,56 +419,65 @@
 
     def fold_early():
         def step(n, carry):
-            fold_send(n, n // 2, 0).start()
+            fold_send(n, n // along_y, 0).start()
             return carry
 
         lax.fori_loop(0, groups, step, 0)
 
-    def fold_mid():
+    def fold_ready():
         ref = fr.at[:, pl.ds(0, early)]
         remote(ref, ref, f_sem.at[0], f_sem.at[1], ynb, dp).wait_recv()
 
-        def step(n, carry):
-            mode = n // 2
-            fold_send(n, mode, 1).wait_recv()
-            bs[n, 0] = (part[n, 2 - mode] + fr[n, 1].astype(f32)).astype(bf16)
-            bs[n, 1] = (part[n, 6 - mode] + fr[n, 3].astype(f32)).astype(bf16)
-            to = znb + mode * (ynb - znb)
-            remote(bs.at[n], br.at[n], b_sem.at[0], b_sem.at[1 + n], to, dp).start()
-            return carry
-
-        lax.fori_loop(0, groups, step, 0)
-
-    def fold_cross():
-        def step(n, carry):
-            remote(bs.at[n], br.at[n], b_sem.at[0], b_sem.at[1 + n], znb, dp).wait_recv()
-            xs[n] = (part[n, 4] + fr[n, 2].astype(f32) + br[n, 1].astype(f32)).astype(bf16)
-            remote(xs.at[n], xr.at[n], x_sem.at[0], x_sem.at[1 + n], twin, dp).start()
-            return carry
-
-        lax.fori_loop(0, groups, step, 0)
+    def fold_mid(n):
+        mode = n // along_y
+        fold_send(n, mode, 1).wait_recv()
+        bs[n, 0] = (part[n, 2 - mode] + fr[n, 1].astype(f32)).astype(bf16)
+        bs[n, 1] = (part[n, 6 - mode] + fr[n, 3].astype(f32)).astype(bf16)
+        remote(bs.at[n], br.at[n], f_sem.at[0], b_sem.at[n], (znb, ynb)[mode], dp).start()
+
+    def fold_cross(n):
+        remote(bs.at[n], br.at[n], f_sem.at[0], b_sem.at[n], znb, dp).wait_recv()
+        xs[n] = (part[n, 4] + fr[n, 2].astype(f32) + br[n, 1].astype(f32)).astype(bf16)
+        remote(xs.at[n], xr.at[n], f_sem.at[0], x_sem.at[0], twin, dp).start()
 
     def pass_hidden(wave):
         block = wave_rows(wave)
         ref = hw_recv.at[1, :, block]
-        remote(ref, ref, h_send.at[0, 1], h_done.at[1 + wave], ep, peers_dp[1]).wait_recv()
-        remote(ref, hw_recv.at[2, :, block], h_send.at[0, 2], h_done.at[3], ep, peers_dp[0]).start()
+        remote(ref, ref, h_send.at[0], h_done.at[1 + wave], ep, peers_dp[1]).wait_recv()
+        remote(ref, hw_recv.at[2, :, block], h_send.at[0], h_done.at[0], ep, peers_dp[0]).start()
 
     def pass_grad_first():
         ref = gp_recv.at[1, :, :, wave_rows(0)]
-        remote(ref, ref, h_send.at[1, 1], h_done.at[5], ep, peers_dp[1]).wait_recv()
-        remote(ref, gp_recv.at[2, :, :, wave_rows(0)], h_send.at[1, 2], h_done.at[6 + tiles], ep, peers_dp[0]).start()
+        remote(ref, ref, h_send.at[1], h_done.at[5], ep, peers_dp[1]).wait_recv()
+        remote(ref, gp_recv.at[2, :, :, wave_rows(0)], h_send.at[1], h_done.at[6 + tiles], ep, peers_dp[0]).start()
 
     def pass_grad(t):
         ref = gp_recv.at[1, t, :, wave_rows(1)]
-        remote(ref, ref, h_send.at[1, 1], h_done.at[6 + t], ep, peers_dp[1]).wait_recv()
+        remote(ref, ref, h_send.at[1], h_done.at[6 + t], ep, peers_dp[1]).wait_recv()
         remote(
-            ref, gp_recv.at[2, t, :, wave_rows(1)], h_send.at[1, 2], h_done.at[7 + tiles + t], ep, peers_dp[0]
+            ref, gp_recv.at[2, t, :, wave_rows(1)], h_send.at[1], h_done.at[7 + tiles + t], ep, peers_dp[0]
         ).start()
 
+    def turn_down():
+        def step(t, carry):
+            for j in range(groups):
+                wdt[pl.ds(j * col, col), span(t, ft)] = wdn[span(t, ft), pl.ds(j * col, col)].T
+            return carry
+
+        lax.fori_loop(0, tiles, step, 0)
+
+    def turn_up():
+        def step(n, carry):
+            for t in range(tiles):
+                wgt[pl.ds(t * ft, ft), span(n, col)] = wg[span(n, col), pl.ds(t * ft, ft)].T
+                wut[pl.ds(t * ft, ft), span(n, col)] = wu[span(n, col), pl.ds(t * ft, ft)].T
+            return carry
+
+        lax.fori_loop(0, groups, step, 0)
+
+    w_loads[2].wait()
+    turn_down()
     pair_out(0)
-    if lead == 4:
-        take(0, 3)
     for load in w_loads[0:2]:
         load.wait()
     remote(wbuf, wbuf, w_sem.at[0], w_sem.at[1], ynb, dp).wait_recv()
@@ -464,90 +489,78 @@
     gate_step(0)
     inner_pass(0, near)
     pair_out(1)
-    if lead == 4:
-        take(1, 3)
-    w_loads[2].wait()
     back_step(0)
     inner_pass(0, far)
-    for r in (1, 2):
-        ref = cols.at[1, r, pl.ds(0, count)]
-        remote(ref, ref, c_send.at[1, r], c_recv.at[1, r], ep, peers_dp[r]).wait_recv()
-    own_out(2)
     slot_step(0)
     inner_pass(1, near)
     inner_pass(1, far)
+    ref = cols.at[1, pl.ds(1, 2), pl.ds(0, count)]
+    remote(ref, ref, c_send.at[0], c_recv.at[2], ep, peers_dp[1]).wait_recv()
+    own_out(2)
     outer_pass(0, near)
+    turn_up()
+    facing_out(2)
     outer_pass(0, far)
     if lead == 3:
         take(0, 3)
     take(0, near + 1)
     outer_pass(1, near)
+    outer_pass(1, far)
+    inner_pass(2, near)
     take(0, far + 1)
+    inner_pass(2, far)
     gate_step(1)
-    outer_pass(1, far)
     fold_early()
-    pair_out(2)
+    outer_pass(2, near)
+    outer_pass(2, far)
     pass_hidden(0)
     if lead == 3:
         take(1, 3)
     take(1, near + 1)
     take(1, far + 1)
     back_step(1)
-    inner_pass(2, near)
+    diag_out(2)
     slot_step(1)
-    pass_grad_first()
     for s in range(1, 8):
         remote(rs.at[s], rr.at[ep], r_sem.at[0], r_sem.at[1], targets[s], dp).start()
     pltpu.make_async_copy(rs.at[0], rr.at[ep], r_sem.at[1]).start()
-    inner_pass(2, far)
-    pass_hidden(1)
+    pass_grad_first()
+    remote(cols.at[0], cols.at[0], c_send.at[0], c_recv.at[0], ep, peers_dp[0]).wait_recv()
     colst[0] = tc[0, dp].T
     for r in range(3):
-        remote(cols.at[0, r], cols.at[0, r], c_send.at[0, r], c_recv.at[0, r], ep, peers_dp[r]).wait_recv()
         colst[1 + r] = cols[0, r].T
-    fold_mid()
-    outer_pass(2, near)
-    outer_pass(2, far)
-    remote(cols.at[1, 0], cols.at[1, 0], c_send.at[1, 0], c_recv.at[1, 0], ep, peers_dp[0]).wait_recv()
-    fold_cross()
-    got(2, 3)
-    got(2, near + 1)
-    got(2, far + 1)
-    remote(hw_recv.at[0], hw_recv.at[0], h_send.at[0, 0], h_done.at[0], ep, peers_dp[0]).wait_recv()
-    remote(hw_recv.at[2], hw_recv.at[2], h_send.at[0, 2], h_done.at[3], ep, peers_dp[0]).wait_recv()
-
-    def down_step(t, carry):
+    pass_hidden(1)
+    fold_ready()
+    fold_mid(0)
+    fold_mid(2)
+    fold_mid(1)
+    fold_mid(3)
+    remote(cols.at[1, 0], cols.at[1, 0], c_send.at[0], c_recv.at[1], ep, peers_dp[0]).wait_recv()
+    remote(gp_recv.at[0], gp_recv.at[0], h_send.at[1], h_done.at[4], ep, peers_dp[0]).wait_recv()
+    ref = gp_recv.at[2, :, :, wave_rows(0)]
+    remote(ref, ref, h_send.at[1], h_done.at[6 + tiles], ep, peers_dp[0]).wait_recv()
+
+    def down_tile(t):
         blocks = [hw_own.at[t]] + [hw_recv.at[r, t] for r in range(3)]
         cots = [tc.at[1, dp]] + [cols.at[1, r] for r in range(3)]
         grad_down = jnp.zeros((ft, col), f32)
         for g in range(4):
             grad_down += lax.dot_general(blocks[g][...], cots[g][...], contract_first, preferred_element_type=f32)
         gd_ref[span(t, ft), :] = grad_down.astype(bf16)
-        return carry
-
-    lax.fori_loop(0, tiles, down_step, 0)
-    remote(gp_recv.at[0], gp_recv.at[0], h_send.at[1, 0], h_done.at[4], ep, peers_dp[0]).wait_recv()
-    ref = gp_recv.at[2, :, :, wave_rows(0)]
-    remote(ref, ref, h_send.at[1, 2], h_done.at[6 + tiles], ep, peers_dp[0]).wait_recv()
-    pass_grad(0)
-
-    def sum_step(n, carry):
-        remote(xs.at[n], xr.at[n], x_sem.at[0], x_sem.at[1 + n], twin, dp).wait_recv()
-        total = part[n, 0] + fr[n, 0].astype(f32) + br[n, 0].astype(f32) + xr[n].astype(f32)
-        gt_ref[:, span(n, col)] = total.astype(bf16)
-        return carry
-
-    def weight_step(t, carry):
-        @pl.when(t + 1 < tiles)
-        def _():
-            pass_grad(t + 1)
-
-        @pl.when(t + 1 == tiles)
-        def _():
-            lax.fori_loop(0, groups, sum_step, 0)
-
+
+    def sum_all():
+        remote(xs, xr, f_sem.at[0], x_sem.at[0], twin, dp).wait_recv()
+
+        def step(n, carry):
+            total = part[n, 0] + fr[n, 0].astype(f32) + br[n, 0].astype(f32) + xr[n].astype(f32)
+            gt_ref[:, span(n, col)] = total.astype(bf16)
+            return carry
+
+        lax.fori_loop(0, groups, step, 0)
+
+    def weight_tile(t):
         ref = gp_recv.at[2, t, :, wave_rows(1)]
-        remote(ref, ref, h_send.at[1, 2], h_done.at[7 + tiles + t], ep, peers_dp[0]).wait_recv()
+        remote(ref, ref, h_send.at[1], h_done.at[7 + tiles + t], ep, peers_dp[0]).wait_recv()
         blocks = [gp_own.at[t]] + [gp_recv.at[r, t] for r in range(3)]
         grad_gate = jnp.zeros((col, ft), f32)
         grad_up = jnp.zeros((col, ft), f32)
@@ -556,9 +569,28 @@
             grad_up += jnp.dot(colst[g], blocks[g][1], preferred_element_type=f32)
         gg_ref[:, span(t, ft)] = grad_gate.astype(bf16)
         gu_ref[:, span(t, ft)] = grad_up.astype(bf16)
-        return carry
-
-    lax.fori_loop(0, tiles, weight_step, 0)
+
+    def down_ready():
+        got(2, 3)
+        got(2, near + 1)
+        got(2, far + 1)
+        ref = hw_recv.at[pl.ds(0, 2)]
+        remote(ref, ref, h_send.at[0], h_done.at[0], ep, peers_dp[0]).wait_recv()
+
+    pass_grad(0)
+    fold_cross(0)
+    fold_cross(2)
+    fold_cross(1)
+    fold_cross(3)
+    pass_grad(1)
+    weight_tile(0)
+    down_ready()
+    for t in range(tiles):
+        down_tile(t)
+    pass_grad(2)
+    weight_tile(1)
+    sum_all()
+    weight_tile(2)
 
     remote(rr, rr, r_sem.at[0], r_sem.at[1], ynb, dp).wait_recv()
     table = jnp.zeros(ids.shape, f32)
@@ -571,37 +603,37 @@
 
     sent(rs.at[pl.ds(0, ep_size - 1)], r_sem.at[0])
     sent(wd.at[pl.ds(0, ep_size - 1)], w_sem.at[0])
-    sent(fs, f_sem.at[0])
-    sent(bs, b_sem.at[0])
-    sent(xs, x_sem.at[0])
-    for k in range(3):
-        def whole(n):
-            return cols.at[1, pl.ds(1, 2), pl.ds(0, n * count)] if k == 2 else tc.at[k, :, pl.ds(0, n * count)]
-
-        sent(whole(3), g_send.at[k, 0])
-
-        @pl.when(inner)
-        def _():
-            sent(whole(6), g_send.at[k, 1])
-
-        @pl.when(outer)
-        def _():
-            sent(whole(2), g_send.at[k, 1])
-
-    for k in range(2):
-        for r in range(3):
-            sent(cols.at[1, r, pl.ds(0, count)] if k == 1 and r > 0 else cols.at[k, r], c_send.at[k, r])
-            sent((hw_recv, gp_recv)[k].at[r], h_send.at[k, r])
+    sent(wdn.at[pl.ds(0, (7 * groups * count * col) // model)], f_sem.at[0])
+    unit = (groups * count * col) // model
+
+    @pl.when(inner)
+    def _():
+        sent(wdn.at[pl.ds(0, 9 * (2 * unit + unit // 2))], g_send.at[0])
+
+    @pl.when(outer)
+    def _():
+        sent(wdn.at[pl.ds(0, 5 * (2 * unit + unit // 2))], g_send.at[0])
+
+    sent(wdn.at[pl.ds(0, (34 * count * col) // model)], c_send.at[0])
+    sent(hw_recv, h_send.at[0])
+    sent(gp_recv, h_send.at[1])
 
 
 def store_kernel(*refs):
     sems = refs[-1]
     each = (len(refs) - 1) // 2
-    copies = [pltpu.make_async_copy(refs[k], refs[each + k], sems.at[k]) for k in range(each)]
+    copies = []
+    for k in range(each):
+        size = refs[k].shape[0]
+        pieces = store_pieces if size % (16 * store_pieces) == 0 else 1
+        step = size // pieces
+        for p in range(pieces):
+            place = pl.ds(p * step, step)
+            copies.append(pltpu.make_async_copy(refs[k].at[place], refs[each + k].at[place], sems.at[k]))
     for copy in copies:
         copy.start()
-    for copy in copies:
-        copy.wait()
+    for k in range(each):
+        pltpu.make_async_copy(refs[k], refs[each + k], sems.at[k]).wait()
 
 
 def fused_body(tokens, cotangent, expert_ids, route_weights, w_gate, w_up, w_down):
@@ -635,6 +667,9 @@
             pltpu.VMEM((model, width), bf16),
             pltpu.VMEM((model, width), bf16),
             pltpu.VMEM((width, model), bf16),
+            pltpu.VMEM((width, model), bf16),
+            pltpu.VMEM((width, model), bf16),
+            pltpu.VMEM((model, width), bf16),
             pltpu.VMEM((2, groups, rows, col), bf16),
             pltpu.VMEM(small, f32),
             pltpu.VMEM(small, f32),
@@ -659,15 +694,15 @@
             pltpu.VMEM(small, f32),
             dma((7,)),
             dma((2,)),
-            dma((3, 2)),
+            dma((1,)),
             dma((3, experts)),
-            dma((2, 3)),
-            dma((2, 3)),
-            dma((2, 3)),
+            dma((1,)),
+            dma((3,)),
+            dma((2,)),
             dma((7 + 2 * tiles,)),
             dma((2 + groups,)),
-            dma((1 + groups,)),
-            dma((1 + groups,)),
+            dma((groups,)),
+            dma((1,)),
             dma((2,)),
         ],
         compiler_params=pltpu.CompilerParams(
@@ -691,7 +726,7 @@
     tok_count, topk = expert_ids.shape
     experts = lax.axis_size("ep")
     whole = 2 * tok_count * topk // experts >= tok_count
-    paired = lax.axis_size("dp") == 4 and experts == 8 and tok_count in (32, 64)
+    paired = lax.axis_size("dp") == 4 and experts == 8 and tok_count == 32
     chosen = fused_body if whole and paired else routed_body
     return chosen(tokens, cotangent, expert_ids, route_weights, w_gate, w_up, w_down)
 

time: 56.8 us -> 52.5 us (0.924)
  Pallas kernels: 56.1 us -> 51.8 us
    pallas_call x1, Pallas kernels: 54.6 us -> 50.3 us  [fused_body(): pl.pallas_call(fused_kernel, name='fused_layer', out_shape=tuple((pltpu.V...]
where the time goes in v3:
time: 52.5 us; the launch traced here: 52.4 us
  Pallas kernels  51.8 us (99%)
  between operations  0.64 us (1%)
    pallas_call x1, Pallas kernels, fused_body(): pl.pallas_call(fused_kernel, name='fused_layer', out_shape=tuple((pltpu.V...  50.3 us
    pallas_call x1, Pallas kernels, fused_body(): pl.pallas_call(store_kernel, name='store_results', out_shape=tuple((jax.S...  1.48 us

profile of v3, /device:TPU:0, one launch (start us, length us, event | category | flops | bytes accessed | tf_op | source)
XLA Modules:
  0.0 52.4 jit_solution(11561643943603355376)
XLA Ops:
  0.6 50.3 %fused_layer.1 = (bf16[32,2048]{1,0:T(8,128)(2,1)S(1)}, bf16[8,32]{1,0:T(8,128)(2,1)S(1)}, bf16[512,768]{1,0:T(8,128)(2,1)S(1)}, bf16[512,768]{1,0:T(8,128)(2,1)S(1)}, bf16[768,512]{1,0:T(8,128)(2,1)S(1)}) custom-call(bf16[32,2048]{1,0:T(8,128)(2,1)} %tok_hbm.1, bf16[32,2048]{1,0:T(8,128)(2,1)} %cot_hbm.1, s32[8,32]{1,0:T(8,128)} %bitcast.12, ...), custom_call_target="tpu_custom_call" | custom-call | tf_op jit(solution)/shard_map/fused_layer/pallas_call | solution.py:658
  50.9 1.5 %store_results.1 = (bf16[32,2048]{1,0:T(8,128)(2,1)}, bf16[8,32]{1,0:T(8,128)(2,1)}, bf16[512,768]{1,0:T(8,128)(2,1)}, bf16[512,768]{1,0:T(8,128)(2,1)}, bf16[768,512]{1,0:T(8,128)(2,1)}) custom-call(bf16[32,2048]{1,0:T(8,128)(2,1)S(1)} %get-tuple-element.15.refs_0_, bf16[8,32]{1,0:T(8,128)(2,1)S(1)} %get-tuple-element.16.refs_1_, ...), custom_call_target="tpu_custom_call" | custom-call | tf_op jit(solution)/shard_map/store_results/pallas_call | solution.py:712

commit v4 on v3

--- a/solution.py
+++ b/solution.py
@@ -283,6 +283,16 @@
         share(k, 2)
         take(k, 1)
 
+    def side_out():
+        @pl.when(inner)
+        def _():
+            hop(0, 1, 7, 1, facing)
+            hop(1, 1, 7, 1, facing)
+
+    def take_side(k):
+        got(k, near + 1)
+        share(k, near + 1)
+
     def facing_out(k):
         @pl.when(inner)
         def _():
@@ -297,19 +307,21 @@
         got(k, 1)
         hop(k, 1, 3, 0, znb)
 
-    def inner_pass(k, slot):
+    def inner_pass(k, slot, sideways=True):
         @pl.when(inner)
         def _():
             got(k, slot)
             hop(k, slot, 10 - slot, 1, znb)
-            hop(k, slot, slot + 1, 1, ynb)
+            if sideways:
+                hop(k, slot, slot + 1, 1, ynb)
             share(k, slot)
 
-    def outer_pass(k, slot):
+    def outer_pass(k, slot, sideways=True):
         @pl.when(outer)
         def _():
             got(k, slot)
-            hop(k, slot, slot + 1, 1, ynb)
+            if sideways:
+                hop(k, slot, slot + 1, 1, ynb)
             share(k, slot)
 
     for s in range(1, 8):
@@ -487,12 +499,13 @@
     for p in range(ep_size):
         wcol[pl.ds(p * count, count), :] = jnp.broadcast_to(turned[0:count, p * step8:p * step8 + 1], (count, 128))
     gate_step(0)
-    inner_pass(0, near)
+    inner_pass(0, near, False)
     pair_out(1)
+    side_out()
     back_step(0)
     inner_pass(0, far)
     slot_step(0)
-    inner_pass(1, near)
+    inner_pass(1, near, False)
     inner_pass(1, far)
     ref = cols.at[1, pl.ds(1, 2), pl.ds(0, count)]
     remote(ref, ref, c_send.at[0], c_recv.at[2], ep, peers_dp[1]).wait_recv()
@@ -503,38 +516,38 @@
     outer_pass(0, far)
     if lead == 3:
         take(0, 3)
-    take(0, near + 1)
+    take_side(0)
     outer_pass(1, near)
     outer_pass(1, far)
-    inner_pass(2, near)
     take(0, far + 1)
-    inner_pass(2, far)
     gate_step(1)
     fold_early()
-    outer_pass(2, near)
-    outer_pass(2, far)
     pass_hidden(0)
     if lead == 3:
         take(1, 3)
-    take(1, near + 1)
+    take_side(1)
     take(1, far + 1)
     back_step(1)
     diag_out(2)
+    inner_pass(2, near)
+    inner_pass(2, far)
     slot_step(1)
     for s in range(1, 8):
         remote(rs.at[s], rr.at[ep], r_sem.at[0], r_sem.at[1], targets[s], dp).start()
     pltpu.make_async_copy(rs.at[0], rr.at[ep], r_sem.at[1]).start()
+    outer_pass(2, near)
+    outer_pass(2, far)
     pass_grad_first()
+    fold_ready()
+    fold_mid(0)
+    fold_mid(2)
     remote(cols.at[0], cols.at[0], c_send.at[0], c_recv.at[0], ep, peers_dp[0]).wait_recv()
     colst[0] = tc[0, dp].T
     for r in range(3):
         colst[1 + r] = cols[0, r].T
-    pass_hidden(1)
-    fold_ready()
-    fold_mid(0)
-    fold_mid(2)
     fold_mid(1)
     fold_mid(3)
+    pass_hidden(1)
     remote(cols.at[1, 0], cols.at[1, 0], c_send.at[0], c_recv.at[1], ep, peers_dp[0]).wait_recv()
     remote(gp_recv.at[0], gp_recv.at[0], h_send.at[1], h_done.at[4], ep, peers_dp[0]).wait_recv()
     ref = gp_recv.at[2, :, :, wave_rows(0)]
@@ -582,15 +595,16 @@
     fold_cross(2)
     fold_cross(1)
     fold_cross(3)
-    pass_grad(1)
+    for t in range(1, tiles - 1):
+        pass_grad(t)
     weight_tile(0)
     down_ready()
     for t in range(tiles):
         down_tile(t)
-    pass_grad(2)
-    weight_tile(1)
+    pass_grad(tiles - 1)
+    for t in range(1, tiles):
+        weight_tile(t)
     sum_all()
-    weight_tile(2)
 
     remote(rr, rr, r_sem.at[0], r_sem.at[1], ynb, dp).wait_recv()
     table = jnp.zeros(ids.shape, f32)
@@ -608,11 +622,11 @@
 
     @pl.when(inner)
     def _():
-        sent(wdn.at[pl.ds(0, 9 * (2 * unit + unit // 2))], g_send.at[0])
+        sent(wdn.at[pl.ds(0, 18 * unit + 9 * unit // 2)], g_send.at[0])
 
     @pl.when(outer)
     def _():
-        sent(wdn.at[pl.ds(0, 5 * (2 * unit + unit // 2))], g_send.at[0])
+        sent(wdn.at[pl.ds(0, 10 * unit + 5 * unit // 2)], g_send.at[0])
 
     sent(wdn.at[pl.ds(0, (34 * count * col) // model)], c_send.at[0])
     sent(hw_recv, h_send.at[0])
@@ -726,7 +740,9 @@
     tok_count, topk = expert_ids.shape
     experts = lax.axis_size("ep")
     whole = 2 * tok_count * topk // experts >= tok_count
+    width = w_gate.shape[2]
     paired = lax.axis_size("dp") == 4 and experts == 8 and tok_count == 32
+    paired = paired and width % 256 == 0 and width >= 24 * tok_count
     chosen = fused_body if whole and paired else routed_body
     return chosen(tokens, cotangent, expert_ids, route_weights, w_gate, w_up, w_down)
 

time: 52.5 us -> 51.6 us (0.983)
  Pallas kernels: 51.8 us -> 50.6 us
    pallas_call x1, Pallas kernels: 50.3 us -> 49.1 us  [fused_body(): pl.pallas_call(fused_kernel, name='fused_layer', out_shape=tuple((pltpu.V...]
where the time goes in v4:
time: 51.6 us; the launch traced here: 51.2 us
  Pallas kernels  50.6 us (98%)
  between operations  0.64 us (1%)
    pallas_call x1, Pallas kernels, fused_body(): pl.pallas_call(fused_kernel, name='fused_layer', out_shape=tuple((pltpu.V...  49.1 us
    pallas_call x1, Pallas kernels, fused_body(): pl.pallas_call(store_kernel, name='store_results', out_shape=tuple((jax.S...  1.48 us

profile of v4, /device:TPU:0, one launch (start us, length us, event | category | flops | bytes accessed | tf_op | source)
XLA Modules:
  0.0 51.2 jit_solution(4230346155727490419)
XLA Ops:
  0.6 49.1 %fused_layer.1 = (bf16[32,2048]{1,0:T(8,128)(2,1)S(1)}, bf16[8,32]{1,0:T(8,128)(2,1)S(1)}, bf16[512,768]{1,0:T(8,128)(2,1)S(1)}, bf16[512,768]{1,0:T(8,128)(2,1)S(1)}, bf16[768,512]{1,0:T(8,128)(2,1)S(1)}) custom-call(bf16[32,2048]{1,0:T(8,128)(2,1)} %tok_hbm.1, bf16[32,2048]{1,0:T(8,128)(2,1)} %cot_hbm.1, s32[8,32]{1,0:T(8,128)} %bitcast.12, ...), custom_call_target="tpu_custom_call" | custom-call | tf_op jit(solution)/shard_map/fused_layer/pallas_call | solution.py:672
  49.8 1.5 %store_results.1 = (bf16[32,2048]{1,0:T(8,128)(2,1)}, bf16[8,32]{1,0:T(8,128)(2,1)}, bf16[512,768]{1,0:T(8,128)(2,1)}, bf16[512,768]{1,0:T(8,128)(2,1)}, bf16[768,512]{1,0:T(8,128)(2,1)}) custom-call(bf16[32,2048]{1,0:T(8,128)(2,1)S(1)} %get-tuple-element.15.refs_0_, bf16[8,32]{1,0:T(8,128)(2,1)S(1)} %get-tuple-element.16.refs_1_, ...), custom_call_target="tpu_custom_call" | custom-call | tf_op jit(solution)/shard_map/store_results/pallas_call | solution.py:726

commit v5 on v4

--- a/solution.py
+++ b/solution.py
@@ -229,6 +229,121 @@
         )
     for peer in peers_dp:
         pl.semaphore_signal(barrier, inc=1, device_id=(ep, peer), device_id_type=pl.DeviceIdType.MESH)
+    pl.semaphore_wait(barrier, ep_size - 1 + len(peers_dp))
+
+    def view(k, slot):
+        place = span(slot, count)
+        return cols.at[1, pl.ds(1, 2), place] if k == 2 else tc.at[k, :, place]
+
+    def hop(k, slot, there, late, ep_to):
+        remote(view(k, slot), view(k, there), g_send.at[0], g_recv.at[k, there], ep_to, dp).start()
+
+    def got(k, slot):
+        remote(view(k, slot), view(k, slot), g_send.at[0], g_recv.at[k, slot], ynb, dp).wait_recv()
+
+    def share(k, slot, every=False):
+        if k == 2:
+            return
+        for r in (1, 2, 0) if k == 0 or every else (0,):
+            peer = peers_dp[r]
+            remote(
+                tc.at[k, peer, span(slot, count)], cols.at[k, r, span(slot, count)],
+                c_send.at[0], c_recv.at[0 if k == 0 else 1 if r == 0 else 2], ep, peer,
+            ).start()
+
+    def take(k, slot):
+        got(k, slot)
+        share(k, slot)
+
+    def own_out(k):
+        hop(k, 0, 1, 0, ynb)
+        hop(k, 0, 2, 0, znb)
+
+        @pl.when(inner)
+        def _():
+            hop(k, 0, 6, 1, facing)
+
+    def pair_out(k):
+        got(k, 2)
+        hop(k, 2, 3, 0, ynb)
+
+        @pl.when(inner)
+        def _():
+            hop(k, 2, 4, 1, facing)
+
+        share(k, 2)
+        take(k, 1)
+
+    def side_out():
+        @pl.when(inner)
+        def _():
+            hop(0, 1, 7, 1, facing)
+            hop(1, 1, 7, 1, facing)
+
+    def half(part, slot):
+        return tc.at[1, pl.ds(part * (groups // 2), groups // 2), span(slot, count)]
+
+    def half_copy(part, slot, there, mark, ep_to):
+        return remote(half(part, slot), half(part, there), g_send.at[0], g_recv.at[1, mark], ep_to, dp)
+
+    def last_pass():
+        @pl.when(outer)
+        def _():
+            got(1, 6)
+            half_copy(0, 6, 7, 7, ynb).start()
+            share(1, 6)
+
+    def last_take():
+        @pl.when(inner)
+        def _():
+            got(1, 5)
+            half_copy(1, 5, 7, 0, znb).start()
+
+        @pl.when(outer)
+        def _():
+            half_copy(0, 7, 7, 7, ynb).wait_recv()
+            half_copy(1, 7, 7, 0, znb).wait_recv()
+
+        share(1, far + 1)
+
+    def take_side(k):
+        got(k, near + 1)
+        share(k, near + 1)
+
+    def facing_out(k):
+        @pl.when(inner)
+        def _():
+            got(k, 2)
+            hop(k, 2, 4, 1, facing)
+
+    def diag_out(k):
+        @pl.when(outer)
+        def _():
+            got(k, 2)
+
+        got(k, 1)
+        hop(k, 1, 3, 0, znb)
+
+    def inner_pass(k, slot, sideways=True):
+        @pl.when(inner)
+        def _():
+            got(k, slot)
+            hop(k, slot, 10 - slot, 1, znb)
+            if sideways:
+                hop(k, slot, slot + 1, 1, ynb)
+            share(k, slot)
+
+    def outer_pass(k, slot, sideways=True):
+        @pl.when(outer)
+        def _():
+            got(k, slot)
+            if sideways:
+                hop(k, slot, slot + 1, 1, ynb)
+            share(k, slot)
+
+    pltpu.make_async_copy(view(0, 0), view(0, 0), l_sem.at[0]).wait()
+    own_out(0)
+    share(0, 0, True)
     wd[...] = jnp.zeros(wd.shape, f32)
     rs[...] = jnp.zeros(rs.shape, f32)
     for load in lists:
@@ -238,100 +353,13 @@
     for e in range(ep_size):
         line = jnp.sum(jnp.where(ids == e, values, 0.0), axis=0, keepdims=True)
         wd[e, :, 0:count] = jnp.broadcast_to(line, (wd.shape[1], count))
-    pl.semaphore_wait(barrier, ep_size - 1 + len(peers_dp))
-
-    def view(k, slot):
-        place = span(slot, count)
-        return cols.at[1, pl.ds(1, 2), place] if k == 2 else tc.at[k, :, place]
-
-    def hop(k, slot, there, late, ep_to):
-        remote(view(k, slot), view(k, there), g_send.at[0], g_recv.at[k, there], ep_to, dp).start()
-
-    def got(k, slot):
-        remote(view(k, slot), view(k, slot), g_send.at[0], g_recv.at[k, slot], ynb, dp).wait_recv()
-
-    def share(k, slot, every=False):
-        if k == 2:
-            return
-        for r in (1, 2, 0) if k == 0 or every else (0,):
-            peer = peers_dp[r]
-            remote(
-                tc.at[k, peer, span(slot, count)], cols.at[k, r, span(slot, count)],
-                c_send.at[0], c_recv.at[0 if k == 0 else 1 if r == 0 else 2], ep, peer,
-            ).start()
-
-    def take(k, slot):
-        got(k, slot)
-        share(k, slot)
-
-    def own_out(k):
-        hop(k, 0, 1, 0, ynb)
-        hop(k, 0, 2, 0, znb)
-
-        @pl.when(inner)
-        def _():
-            hop(k, 0, 6, 1, facing)
-
-    def pair_out(k):
-        got(k, 2)
-        hop(k, 2, 3, 0, ynb)
-
-        @pl.when(inner)
-        def _():
-            hop(k, 2, 4, 1, facing)
-
-        share(k, 2)
-        take(k, 1)
-
-    def side_out():
-        @pl.when(inner)
-        def _():
-            hop(0, 1, 7, 1, facing)
-            hop(1, 1, 7, 1, facing)
-
-    def take_side(k):
-        got(k, near + 1)
-        share(k, near + 1)
-
-    def facing_out(k):
-        @pl.when(inner)
-        def _():
-            got(k, 2)
-            hop(k, 2, 4, 1, facing)
-
-    def diag_out(k):
-        @pl.when(outer)
-        def _():
-            got(k, 2)
-
-        got(k, 1)
-        hop(k, 1, 3, 0, znb)
-
-    def inner_pass(k, slot, sideways=True):
-        @pl.when(inner)
-        def _():
-            got(k, slot)
-            hop(k, slot, 10 - slot, 1, znb)
-            if sideways:
-                hop(k, slot, slot + 1, 1, ynb)
-            share(k, slot)
-
-    def outer_pass(k, slot, sideways=True):
-        @pl.when(outer)
-        def _():
-            got(k, slot)
-            if sideways:
-                hop(k, slot, slot + 1, 1, ynb)
-            share(k, slot)
-
     for s in range(1, 8):
-        remote(wd.at[targets[s]], wbuf.at[s], w_sem.at[0], w_sem.at[1], targets[s], dp).start()
+        remote(wd.at[targets[s]], wbuf.at[s], w_sem.at[0], w_sem.at[1 if s < lead else 2], targets[s], dp).start()
     keep_w = pltpu.make_async_copy(wd.at[ep], wbuf.at[0], w_sem.at[1])
     keep_w.start()
-    for k in range(2):
-        pltpu.make_async_copy(view(k, 0), view(k, 0), l_sem.at[k]).wait()
-        own_out(k)
-        share(k, 0, True)
+    pltpu.make_async_copy(view(1, 0), view(1, 0), l_sem.at[1]).wait()
+    own_out(1)
+    share(1, 0, True)
 
     def wave_rows(wave):
         return pl.ds(starts[wave] * count, sizes[wave] * count)
@@ -429,12 +457,14 @@
 
         lax.fori_loop(0, groups, step, 0)
 
-    def fold_early():
-        def step(n, carry):
-            fold_send(n, n // along_y, 0).start()
-            return carry
-
-        lax.fori_loop(0, groups, step, 0)
+    def fold_early(where):
+        @pl.when(where)
+        def _():
+            def step(n, carry):
+                fold_send(n, n // along_y, 0).start()
+                return carry
+
+            lax.fori_loop(0, groups, step, 0)
 
     def fold_ready():
         ref = fr.at[:, pl.ds(0, early)]
@@ -470,6 +500,17 @@
             ref, gp_recv.at[2, t, :, wave_rows(1)], h_send.at[1], h_done.at[7 + tiles + t], ep, peers_dp[0]
         ).start()
 
+    def take_weights(wave):
+        start, size = starts[wave], sizes[wave]
+        ref = wbuf.at[pl.ds(start, size)]
+        remote(ref, ref, w_sem.at[0], w_sem.at[1 + wave], ynb, dp).wait_recv()
+        step = wbuf.shape[1]
+        flat = wbuf[start:start + size].reshape(size * step, wbuf.shape[2])
+        turned = jnp.concatenate([flat, jnp.zeros((128 - size * step, wbuf.shape[2]), f32)], axis=0).T
+        for p in range(size):
+            line = turned[0:count, p * step:p * step + 1]
+            wcol[pl.ds((start + p) * count, count), :] = jnp.broadcast_to(line, (count, 128))
+
     def turn_down():
         def step(t, carry):
             for j in range(groups):
@@ -492,12 +533,7 @@
     pair_out(0)
     for load in w_loads[0:2]:
         load.wait()
-    remote(wbuf, wbuf, w_sem.at[0], w_sem.at[1], ynb, dp).wait_recv()
-    flat = wbuf[...].reshape(ep_size * wbuf.shape[1], wbuf.shape[2])
-    turned = jnp.concatenate([flat] * (128 // flat.shape[0]), axis=0).T
-    step8 = wbuf.shape[1]
-    for p in range(ep_size):
-        wcol[pl.ds(p * count, count), :] = jnp.broadcast_to(turned[0:count, p * step8:p * step8 + 1], (count, 128))
+    take_weights(0)
     gate_step(0)
     inner_pass(0, near, False)
     pair_out(1)
@@ -518,15 +554,17 @@
         take(0, 3)
     take_side(0)
     outer_pass(1, near)
-    outer_pass(1, far)
+    last_pass()
     take(0, far + 1)
+    take_weights(1)
     gate_step(1)
-    fold_early()
+    fold_early(outer)
     pass_hidden(0)
     if lead == 3:
         take(1, 3)
     take_side(1)
-    take(1, far + 1)
+    last_take()
+    fold_early(inner)
     back_step(1)
     diag_out(2)
     inner_pass(2, near)
@@ -622,11 +660,11 @@
 
     @pl.when(inner)
     def _():
-        sent(wdn.at[pl.ds(0, 18 * unit + 9 * unit // 2)], g_send.at[0])
+        sent(wdn.at[pl.ds(0, 18 * unit + 10 * unit // 2)], g_send.at[0])
 
     @pl.when(outer)
     def _():
-        sent(wdn.at[pl.ds(0, 10 * unit + 5 * unit // 2)], g_send.at[0])
+        sent(wdn.at[pl.ds(0, 10 * unit + 4 * unit // 2)], g_send.at[0])
 
     sent(wdn.at[pl.ds(0, (34 * count * col) // model)], c_send.at[0])
     sent(hw_recv, h_send.at[0])
@@ -707,7 +745,7 @@
             pltpu.VMEM(small, f32),
             pltpu.VMEM(small, f32),
             dma((7,)),
-            dma((2,)),
+            dma((3,)),
             dma((1,)),
             dma((3, experts)),
             dma((1,)),

time: 51.6 us -> 50.9 us (0.986)
  Pallas kernels: 50.6 us -> 49.9 us
    pallas_call x1, Pallas kernels: 49.1 us -> 48.5 us  [fused_body(): pl.pallas_call(fused_kernel, name='fused_layer', out_shape=tuple((pltpu.V...]
where the time goes in v5:
time: 50.9 us; the launch traced here: 50.6 us
  Pallas kernels  49.9 us (98%)
  between operations  0.64 us (1%)
    pallas_call x1, Pallas kernels, fused_body(): pl.pallas_call(fused_kernel, name='fused_layer', out_shape=tuple((pltpu.V...  48.5 us
    pallas_call x1, Pallas kernels, fused_body(): pl.pallas_call(store_kernel, name='store_results', out_shape=tuple((jax.S...  1.48 us

profile of v5, /device:TPU:0, one launch (start us, length us, event | category | flops | bytes accessed | tf_op | source)
XLA Modules:
  0.0 50.6 jit_solution(7409289262464830119)
XLA Ops:
  0.6 48.5 %fused_layer.1 = (bf16[32,2048]{1,0:T(8,128)(2,1)S(1)}, bf16[8,32]{1,0:T(8,128)(2,1)S(1)}, bf16[512,768]{1,0:T(8,128)(2,1)S(1)}, bf16[512,768]{1,0:T(8,128)(2,1)S(1)}, bf16[768,512]{1,0:T(8,128)(2,1)S(1)}) custom-call(bf16[32,2048]{1,0:T(8,128)(2,1)} %tok_hbm.1, bf16[32,2048]{1,0:T(8,128)(2,1)} %cot_hbm.1, s32[8,32]{1,0:T(8,128)} %bitcast.12, ...), custom_call_target="tpu_custom_call" | custom-call | tf_op jit(solution)/shard_map/fused_layer/pallas_call | solution.py:710
  49.1 1.5 %store_results.1 = (bf16[32,2048]{1,0:T(8,128)(2,1)}, bf16[8,32]{1,0:T(8,128)(2,1)}, bf16[512,768]{1,0:T(8,128)(2,1)}, bf16[512,768]{1,0:T(8,128)(2,1)}, bf16[768,512]{1,0:T(8,128)(2,1)}) custom-call(bf16[32,2048]{1,0:T(8,128)(2,1)S(1)} %get-tuple-element.15.refs_0_, bf16[8,32]{1,0:T(8,128)(2,1)S(1)} %get-tuple-element.16.refs_1_, ...), custom_call_target="tpu_custom_call" | custom-call | tf_op jit(solution)/shard_map/store_results/pallas_call | solution.py:764

commit v6 on v5

--- a/solution.py
+++ b/solution.py
@@ -545,7 +545,10 @@
     inner_pass(1, far)
     ref = cols.at[1, pl.ds(1, 2), pl.ds(0, count)]
     remote(ref, ref, c_send.at[0], c_recv.at[2], ep, peers_dp[1]).wait_recv()
-    own_out(2)
+    @pl.when(outer)
+    def _():
+        own_out(2)
+
     outer_pass(0, near)
     turn_up()
     facing_out(2)
@@ -564,6 +567,11 @@
         take(1, 3)
     take_side(1)
     last_take()
+
+    @pl.when(inner)
+    def _():
+        own_out(2)
+
     fold_early(inner)
     back_step(1)
     diag_out(2)

time: 50.9 us -> 50.9 us (level)
  no operation moved by 1% of the time
where the time goes in v6:
time: 50.9 us; the launch traced here: 50.6 us
  Pallas kernels  49.9 us (98%)
  between operations  0.64 us (1%)
    pallas_call x1, Pallas kernels, fused_body(): pl.pallas_call(fused_kernel, name='fused_layer', out_shape=tuple((pltpu.V...  48.5 us
    pallas_call x1, Pallas kernels, fused_body(): pl.pallas_call(store_kernel, name='store_results', out_shape=tuple((jax.S...  1.48 us

profile of v6, /device:TPU:0, one launch (start us, length us, event | category | flops | bytes accessed | tf_op | source)
XLA Modules:
  0.0 50.6 jit_solution(60403802752151985)
XLA Ops:
  0.6 48.5 %fused_layer.1 = (bf16[32,2048]{1,0:T(8,128)(2,1)S(1)}, bf16[8,32]{1,0:T(8,128)(2,1)S(1)}, bf16[512,768]{1,0:T(8,128)(2,1)S(1)}, bf16[512,768]{1,0:T(8,128)(2,1)S(1)}, bf16[768,512]{1,0:T(8,128)(2,1)S(1)}) custom-call(bf16[32,2048]{1,0:T(8,128)(2,1)} %tok_hbm.1, bf16[32,2048]{1,0:T(8,128)(2,1)} %cot_hbm.1, s32[8,32]{1,0:T(8,128)} %bitcast.12, ...), custom_call_target="tpu_custom_call" | custom-call | tf_op jit(solution)/shard_map/fused_layer/pallas_call | solution.py:718
  49.1 1.5 %store_results.1 = (bf16[32,2048]{1,0:T(8,128)(2,1)}, bf16[8,32]{1,0:T(8,128)(2,1)}, bf16[512,768]{1,0:T(8,128)(2,1)}, bf16[512,768]{1,0:T(8,128)(2,1)}, bf16[768,512]{1,0:T(8,128)(2,1)}) custom-call(bf16[32,2048]{1,0:T(8,128)(2,1)S(1)} %get-tuple-element.15.refs_0_, bf16[8,32]{1,0:T(8,128)(2,1)S(1)} %get-tuple-element.16.refs_1_, ...), custom_call_target="tpu_custom_call" | custom-call | tf_op jit(solution)/shard_map/store_results/pallas_call | solution.py:772
